TPU v7x, 256 devices: a whole 4x4x8 slice. The times are simulated.
256 devices in a mesh: row: 16 (over x, y), col: 16 (over z, core).
Axes of the slice: x: 4, y: 4, z: 8, core: 2. Of those that a mesh axis runs over, the one named last changes fastest.
Arguments:
- fixed_section: bfloat16 [512, 2048], P('row', 'col'), may hold values from -6 to 6
- moving_section: bfloat16 [512, 2048], P('row', 'col'), may hold values from -6 to 6
- field_init: float32 [2, 512, 2048], P(None, 'row', 'col'), may hold values from -48 to 48
- first_weight: float32 [8, 9], replicated, may hold values from -2 to 2
- first_bias: float32 [8], replicated, may hold values from -0.5 to 0.5
- second_weight: float32 [8, 8, 9], replicated, may hold values from -0.75 to 0.75
Outputs:
- field_change: float32 [2, 512, 2048], P(None, 'row', 'col')
All inputs are finite; a program needn't handle non-finite values.
Results may differ from a plain program's by a relative error of at most 0.011.
Values may be sent and summed in bfloat16 or wider, within the bound.
A program may use at most 64 MiB of HBM per device.

v0:
```python
import jax
import jax.numpy as jnp
from jax import lax
from jax.sharding import PartitionSpec as P

REACH = 16
ITERS = 3


stiffness = 0.01
step_size = 0.5
adam_epsilon = 0.01


def extended(x, sides, width):
    for axis, dim in sides:
        peers, length = (lax.axis_size(axis), x.shape[dim])
        up = [(i, (i + 1) % peers) for i in range(peers - 1)]
        down = [(j, i) for i, j in up]
        last = lax.slice_in_dim(x, length - width, length, axis=dim)
        leading = lax.slice_in_dim(x, 0, width, axis=dim)
        before = lax.ppermute(last, axis, up)
        after = lax.ppermute(leading, axis, down)
        x = jnp.concatenate([before, x, after], axis=dim)
    return x


def encode(image_ext, first_weight, first_bias, second_weight, first_mask):
    out_rows = image_ext.shape[0] - 2
    out_cols = image_ext.shape[1] - 2
    hidden = (
        jnp.zeros((first_weight.shape[0], out_rows, out_cols), jnp.float32)
        + first_bias[:, None, None]
    )
    for tap_index in range(9):
        tap_row = tap_index // 3
        tap_col = tap_index % 3
        hidden = (
            hidden
            + first_weight[:, tap_index, None, None]
            * image_ext[None, tap_row : tap_row + out_rows, tap_col : tap_col + out_cols]
        )
    hidden = jnp.maximum(hidden, 0.0) * first_mask
    out_rows = out_rows - 2
    out_cols = out_cols - 2
    embedding = jnp.zeros((second_weight.shape[0], out_rows, out_cols), jnp.float32)
    for tap_index in range(9):
        tap_row = tap_index // 3
        tap_col = tap_index % 3
        embedding = embedding + jnp.einsum(
            "oc,chw->ohw",
            second_weight[:, :, tap_index],
            hidden[:, tap_row : tap_row + out_rows, tap_col : tap_col + out_cols],
            precision=lax.Precision.HIGHEST,
        )
    return embedding


def sample(flattened, ext_cols, displace, margin, fixed_embedding):
    channels = fixed_embedding.shape[0]
    out_rows = displace.shape[1]
    out_cols = displace.shape[2]
    nearest = jnp.floor(displace + 0.5)
    fraction = displace - nearest
    offsets = nearest.astype(jnp.int32)
    spline = [0.5 * (0.5 - fraction) ** 2, 0.75 - fraction * fraction, 0.5 * (0.5 + fraction) ** 2]
    slopes = [fraction - 0.5, -2.0 * fraction, 0.5 + fraction]
    base_row = lax.broadcasted_iota(jnp.int32, (out_rows, out_cols), 0) + margin + offsets[0]
    base_col = lax.broadcasted_iota(jnp.int32, (out_rows, out_cols), 1) + margin + offsets[1]
    warped = jnp.zeros((channels, out_rows, out_cols), jnp.float32)
    along_row = jnp.zeros((channels, out_rows, out_cols), jnp.float32)
    along_col = jnp.zeros((channels, out_rows, out_cols), jnp.float32)
    for tap_row in range(3):
        for tap_col in range(3):
            position = (base_row + (tap_row - 1)) * ext_cols + base_col + (tap_col - 1)
            picked = jnp.take(flattened, position.reshape(-1), axis=1).reshape(
                channels, out_rows, out_cols
            )
            warped = warped + (spline[tap_row][0] * spline[tap_col][1])[None] * picked
            along_row = along_row + (slopes[tap_row][0] * spline[tap_col][1])[None] * picked
            along_col = along_col + (spline[tap_row][0] * slopes[tap_col][1])[None] * picked
    mismatch = warped - fixed_embedding
    factor = 2.0 / channels
    return jnp.stack(
        [
            jnp.sum(mismatch * along_row, axis=0) * factor,
            jnp.sum(mismatch * along_col, axis=0) * factor,
        ]
    )


def section_mask(start_row, start_col, full_rows, full_cols, tile_rows, tile_cols, width):
    shape_ext = (tile_rows + 2 * width, tile_cols + 2 * width)
    global_row = start_row - width + lax.broadcasted_iota(jnp.int32, shape_ext, 0)
    global_col = start_col - width + lax.broadcasted_iota(jnp.int32, shape_ext, 1)
    return (
        (global_row >= 0) & (global_row < full_rows) & (global_col >= 0) & (global_col < full_cols)
    ).astype(jnp.float32)


def local(fixed_section, moving_section, field_init, first_weight, first_bias, second_weight):
    tile_rows, tile_cols = fixed_section.shape
    margin = REACH + 1
    start_row = lax.axis_index("row") * tile_rows
    start_col = lax.axis_index("col") * tile_cols
    full_rows = tile_rows * lax.axis_size("row")
    full_cols = tile_cols * lax.axis_size("col")

    def inside(width):
        return section_mask(start_row, start_col, full_rows, full_cols, tile_rows, tile_cols, width)

    fixed_ext, moving_ext = (
        extended(fixed_section, (("row", 0), ("col", 1)), 2),
        extended(moving_section, (("row", 0), ("col", 1)), 2),
    )
    fixed_embedding = encode(
        fixed_ext.astype(jnp.float32), first_weight, first_bias, second_weight, inside(1)
    )
    moving_local = encode(
        moving_ext.astype(jnp.float32), first_weight, first_bias, second_weight, inside(1)
    )
    moving_embedding = extended(moving_local, (("row", 1), ("col", 2)), margin)
    channels, ext_rows, ext_cols = moving_embedding.shape
    flattened = moving_embedding.reshape(channels, ext_rows * ext_cols)
    raw_field = field_init
    first_moment = jnp.zeros_like(field_init)
    second_moment = jnp.zeros_like(field_init)
    for iteration in range(ITERS):
        squashed = jnp.tanh(raw_field / REACH)
        displace = REACH * squashed
        data_term = sample(flattened, ext_cols, displace, margin, fixed_embedding)
        padded = extended(displace, (("row", 1), ("col", 2)), 1)
        neighbours = (
            padded[:, 2:, 1:-1] + padded[:, :-2, 1:-1] + padded[:, 1:-1, 2:] + padded[:, 1:-1, :-2]
        )
        gradient = (data_term + 2.0 * stiffness * (4.0 * displace - neighbours)) * (
            1.0 - squashed * squashed
        )
        first_moment = 0.9 * first_moment + 0.1 * gradient
        second_moment = 0.999 * second_moment + 0.001 * gradient * gradient
        corrected_one = first_moment / (1.0 - 0.9 ** (iteration + 1))
        corrected_two = second_moment / (1.0 - 0.999 ** (iteration + 1))
        raw_field = raw_field - step_size * corrected_one / (jnp.sqrt(corrected_two) + adam_epsilon)
    return raw_field - field_init


def solution(mesh):
    return jax.shard_map(
        local,
        mesh=mesh,
        in_specs=(P("row", "col"), P("row", "col"), P(None, "row", "col"), P(), P(), P()),
        out_specs=P(None, "row", "col"),
        check_vma=False,
    )
```

profile of v0, /device:TPU:121, one launch (start us, length us, event | category | flops | bytes accessed | tf_op | source)
XLA Modules:
  0.0 696.4 jit_solution(3759167863239481832)
XLA Ops:
  3.2 5.0 collective-permute-start.13
  10.9 5.5 collective-permute-start
  26.4 5.5 collective-permute-start.8
  32.0 4.3 collective-permute-start.3
  36.2 4.7 collective-permute-start.2
  42.9 4.9 collective-permute-start.10
  53.0 5.5 collective-permute-start.4
  64.2 4.9 collective-permute-start.6
  78.5 16.8 %gather_fusion.8 = f32[4096,8]{1,0:T(8,128)} fusion(f32[8,10692]{0,1:T(8,128)} %copy.26, s32[4096]{0:T(1024)S(1)} %get-tuple-element.292), kind=kCustom, calls=%fused_computation.8.clone | custom fusion | bytes 278528 | tf_op jit(solution)/shard_map/jit(_take)/gather | solution.py:76
  95.3 3.6 broadcast_select_fusion.18
  99.5 16.8 %gather_fusion.7 = f32[4096,8]{1,0:T(8,128)} fusion(f32[8,10692]{0,1:T(8,128)} %copy.26, s32[4096]{0:T(1024)S(1)} %get-tuple-element.291), kind=kCustom, calls=%fused_computation.7.clone | custom fusion | bytes 278528 | tf_op jit(solution)/shard_map/jit(_take)/gather | solution.py:76
  120.4 16.8 %gather_fusion.6 = f32[4096,8]{1,0:T(8,128)} fusion(f32[8,10692]{0,1:T(8,128)} %copy.26, s32[4096]{0:T(1024)S(1)} %get-tuple-element.290), kind=kCustom, calls=%fused_computation.6.clone | custom fusion | bytes 278528 | tf_op jit(solution)/shard_map/jit(_take)/gather | solution.py:76
  137.2 3.6 broadcast_select_fusion.20
  141.4 16.8 %gather_fusion.5 = f32[4096,8]{1,0:T(8,128)} fusion(f32[8,10692]{0,1:T(8,128)} %copy.26, s32[4096]{0:T(1024)S(1)} %get-tuple-element.309), kind=kCustom, calls=%fused_computation.5.clone | custom fusion | bytes 278528 | tf_op jit(solution)/shard_map/jit(_take)/gather | solution.py:76
  158.2 3.6 broadcast_select_fusion.21
  162.4 16.8 %gather_fusion.4 = f32[4096,8]{1,0:T(8,128)} fusion(f32[8,10692]{0,1:T(8,128)} %copy.26, s32[4096]{0:T(1024)S(1)} %get-tuple-element.310), kind=kCustom, calls=%fused_computation.4.clone | custom fusion | bytes 278528 | tf_op jit(solution)/shard_map/jit(_take)/gather | solution.py:76
  179.1 3.6 broadcast_select_fusion.22
  183.3 16.8 %gather_fusion.3 = f32[4096,8]{1,0:T(8,128)} fusion(f32[8,10692]{0,1:T(8,128)} %copy.26, s32[4096]{0:T(1024)S(1)} %get-tuple-element.311), kind=kCustom, calls=%fused_computation.3.clone | custom fusion | bytes 278528 | tf_op jit(solution)/shard_map/jit(_take)/gather | solution.py:76
  204.3 16.8 %gather_fusion.2 = f32[4096,8]{1,0:T(8,128)} fusion(f32[8,10692]{0,1:T(8,128)} %copy.26, s32[4096]{0:T(1024)S(1)} %get-tuple-element.282), kind=kCustom, calls=%fused_computation.2.clone | custom fusion | bytes 278528 | tf_op jit(solution)/shard_map/jit(_take)/gather | solution.py:76
  221.1 3.6 broadcast_select_fusion.24
  225.3 16.8 %gather_fusion.1 = f32[4096,8]{1,0:T(8,128)} fusion(f32[8,10692]{0,1:T(8,128)} %copy.26, s32[4096]{0:T(1024)S(1)} %get-tuple-element.281), kind=kCustom, calls=%fused_computation.1.clone | custom fusion | bytes 278528 | tf_op jit(solution)/shard_map/jit(_take)/gather | solution.py:76
  246.4 16.8 %gather_fusion = f32[4096,8]{1,0:T(8,128)} fusion(f32[8,10692]{0,1:T(8,128)} %copy.26, s32[4096]{0:T(1024)S(1)} %copy-done.7), kind=kCustom, calls=%fused_computation.clone | custom fusion | bytes 278528 | tf_op jit(solution)/shard_map/jit(_take)/gather | solution.py:76
  263.1 3.6 broadcast_select_fusion.26
  276.0 5.5 collective-permute-start.17
  281.5 16.9 %gather_fusion.17 = f32[4096,8]{1,0:T(8,128)} fusion(f32[8,10692]{0,1:T(8,128)} %copy.26, s32[4096]{0:T(1024)S(1)} %get-tuple-element.277), kind=kCustom, calls=%fused_computation.17.clone | custom fusion | bytes 278528 | tf_op jit(solution)/shard_map/jit(_take)/gather | solution.py:76
  302.6 16.8 %gather_fusion.16 = f32[4096,8]{1,0:T(8,128)} fusion(f32[8,10692]{0,1:T(8,128)} %copy.26, s32[4096]{0:T(1024)S(1)} %get-tuple-element.276), kind=kCustom, calls=%fused_computation.16.clone | custom fusion | bytes 278528 | tf_op jit(solution)/shard_map/jit(_take)/gather | solution.py:76
  323.6 16.8 %gather_fusion.15 = f32[4096,8]{1,0:T(8,128)} fusion(f32[8,10692]{0,1:T(8,128)} %copy.26, s32[4096]{0:T(1024)S(1)} %get-tuple-element.275), kind=kCustom, calls=%fused_computation.15.clone | custom fusion | bytes 278528 | tf_op jit(solution)/shard_map/jit(_take)/gather | solution.py:76
  344.5 16.8 %gather_fusion.14 = f32[4096,8]{1,0:T(8,128)} fusion(f32[8,10692]{0,1:T(8,128)} %copy.26, s32[4096]{0:T(1024)S(1)} %get-tuple-element.272), kind=kCustom, calls=%fused_computation.14.clone | custom fusion | bytes 278528 | tf_op jit(solution)/shard_map/jit(_take)/gather | solution.py:76
  361.3 3.6 broadcast_select_fusion.12
  365.5 16.8 %gather_fusion.13 = f32[4096,8]{1,0:T(8,128)} fusion(f32[8,10692]{0,1:T(8,128)} %copy.26, s32[4096]{0:T(1024)S(1)} %get-tuple-element.271), kind=kCustom, calls=%fused_computation.13.clone | custom fusion | bytes 278528 | tf_op jit(solution)/shard_map/jit(_take)/gather | solution.py:76
  386.5 16.8 %gather_fusion.12 = f32[4096,8]{1,0:T(8,128)} fusion(f32[8,10692]{0,1:T(8,128)} %copy.26, s32[4096]{0:T(1024)S(1)} %get-tuple-element.270), kind=kCustom, calls=%fused_computation.12.clone | custom fusion | bytes 278528 | tf_op jit(solution)/shard_map/jit(_take)/gather | solution.py:76
  407.4 16.8 %gather_fusion.11 = f32[4096,8]{1,0:T(8,128)} fusion(f32[8,10692]{0,1:T(8,128)} %copy.26, s32[4096]{0:T(1024)S(1)} %get-tuple-element.267), kind=kCustom, calls=%fused_computation.11.clone | custom fusion | bytes 278528 | tf_op jit(solution)/shard_map/jit(_take)/gather | solution.py:76
  428.4 16.8 %gather_fusion.10 = f32[4096,8]{1,0:T(8,128)} fusion(f32[8,10692]{0,1:T(8,128)} %copy.26, s32[4096]{0:T(1024)S(1)} %get-tuple-element.266), kind=kCustom, calls=%fused_computation.10.clone | custom fusion | bytes 278528 | tf_op jit(solution)/shard_map/jit(_take)/gather | solution.py:76
  449.3 16.8 %gather_fusion.9 = f32[4096,8]{1,0:T(8,128)} fusion(f32[8,10692]{0,1:T(8,128)} %copy.26, s32[4096]{0:T(1024)S(1)} %get-tuple-element.265), kind=kCustom, calls=%fused_computation.9.clone | custom fusion | bytes 278528 | tf_op jit(solution)/shard_map/jit(_take)/gather | solution.py:76
  473.4 4.9 collective-permute-start.19
  480.3 4.6 collective-permute-done.18
  489.1 5.5 collective-permute-start.21
  494.5 17.0 %gather_fusion.26 = f32[4096,8]{1,0:T(8,128)} fusion(f32[8,10692]{0,1:T(8,128)} %copy.26, s32[4096]{0:T(1024)S(1)} %get-tuple-element.262), kind=kCustom, calls=%fused_computation.26.clone | custom fusion | bytes 278528 | tf_op jit(solution)/shard_map/jit(_take)/gather | solution.py:76
  515.7 16.8 %gather_fusion.25 = f32[4096,8]{1,0:T(8,128)} fusion(f32[8,10692]{0,1:T(8,128)} %copy.26, s32[4096]{0:T(1024)S(1)} %get-tuple-element.261), kind=kCustom, calls=%fused_computation.25.clone | custom fusion | bytes 278528 | tf_op jit(solution)/shard_map/jit(_take)/gather | solution.py:76
  536.6 16.8 %gather_fusion.24 = f32[4096,8]{1,0:T(8,128)} fusion(f32[8,10692]{0,1:T(8,128)} %copy.26, s32[4096]{0:T(1024)S(1)} %get-tuple-element.260), kind=kCustom, calls=%fused_computation.24.clone | custom fusion | bytes 278528 | tf_op jit(solution)/shard_map/jit(_take)/gather | solution.py:76
  557.6 16.8 %gather_fusion.23 = f32[4096,8]{1,0:T(8,128)} fusion(f32[8,10692]{0,1:T(8,128)} %copy.26, s32[4096]{0:T(1024)S(1)} %get-tuple-element.257), kind=kCustom, calls=%fused_computation.23.clone | custom fusion | bytes 278528 | tf_op jit(solution)/shard_map/jit(_take)/gather | solution.py:76
  574.4 3.6 broadcast_select_fusion.3
  578.6 16.8 %gather_fusion.22 = f32[4096,8]{1,0:T(8,128)} fusion(f32[8,10692]{0,1:T(8,128)} %copy.26, s32[4096]{0:T(1024)S(1)} %get-tuple-element.256), kind=kCustom, calls=%fused_computation.22.clone | custom fusion | bytes 278528 | tf_op jit(solution)/shard_map/jit(_take)/gather | solution.py:76
  599.5 16.8 %gather_fusion.21 = f32[4096,8]{1,0:T(8,128)} fusion(f32[8,10692]{0,1:T(8,128)} %copy.26, s32[4096]{0:T(1024)S(1)} %get-tuple-element.255), kind=kCustom, calls=%fused_computation.21.clone | custom fusion | bytes 278528 | tf_op jit(solution)/shard_map/jit(_take)/gather | solution.py:76
  620.5 16.8 %gather_fusion.20 = f32[4096,8]{1,0:T(8,128)} fusion(f32[8,10692]{0,1:T(8,128)} %copy.26, s32[4096]{0:T(1024)S(1)} %get-tuple-element.252), kind=kCustom, calls=%fused_computation.20.clone | custom fusion | bytes 278528 | tf_op jit(solution)/shard_map/jit(_take)/gather | solution.py:76
  641.4 16.8 %gather_fusion.19 = f32[4096,8]{1,0:T(8,128)} fusion(f32[8,10692]{0,1:T(8,128)} %copy.26, s32[4096]{0:T(1024)S(1)} %get-tuple-element.251), kind=kCustom, calls=%fused_computation.19.clone | custom fusion | bytes 278528 | tf_op jit(solution)/shard_map/jit(_take)/gather | solution.py:76
  662.4 16.8 %gather_fusion.18 = f32[4096,8]{1,0:T(8,128)} fusion(f32[8,10692]{0,1:T(8,128)} %copy.26, s32[4096]{0:T(1024)S(1)} %get-tuple-element.250), kind=kCustom, calls=%fused_computation.18.clone | custom fusion | bytes 278528 | tf_op jit(solution)/shard_map/jit(_take)/gather | solution.py:76
  690.9 4.6 collective-permute-done.22
  (234 shorter events, 147.5 us)
Async XLA Ops:
  0.0 31.9 %copy-start.8 = (bf16[32,128]{1,0:T(8,128)(2,1)S(1)}, bf16[32,128]{1,0:T(8,128)(2,1)}, u32[]{:S(2)}) copy-start(bf16[32,128]{1,0:T(8,128)(2,1)} %param.9) | copy-start | bytes 24580
  0.0 40.9 %copy-start.9 = (bf16[32,128]{1,0:T(8,128)(2,1)S(1)}, bf16[32,128]{1,0:T(8,128)(2,1)}, u32[]{:S(2)}) copy-start(bf16[32,128]{1,0:T(8,128)(2,1)} %param.8) | copy-start | bytes 24580
  0.0 48.0 %copy-start.22 = (f32[8]{0:T(128)S(1)}, f32[8]{0:T(128)}, u32[]{:S(2)}) copy-start(f32[8]{0:T(128)} %param.12) | copy-start | bytes 100
  0.8 61.2 %copy-start = (f32[2,32,128]{2,1,0:T(8,128)}, f32[2,32,128]{2,1,0:T(8,128)S(1)}, u32[]{:S(2)}) copy-start(f32[2,32,128]{2,1,0:T(8,128)S(1)} %get-tuple-element.238) | copy-start | bytes 98308
  0.9 61.1 %collective-permute-start.12 = (f32[2,1,128]{2,1,0:T(1,128)S(1)}, f32[2,1,128]{2,1,0:T(1,128)S(1)}, u32[]{:S(2)}, u32[]{:S(2)}) collective-permute-start(f32[2,1,128]{2,1,0:T(1,128)S(1)} %get-tuple-element.249), channel_id=1, source_target_pairs={{16,0},{32,16},{48,32},{64,48},{80,64},{96,80},{112,96},{128,112},... | collective-permute-start | bytes 3080 | tf_op jit(solution)/shard_map/ppermute | solution.py:23
  3.2 58.8 %collective-permute-start.13 = (f32[2,1,128]{2,1,0:T(1,128)S(1)}, f32[2,1,128]{2,1,0:T(1,128)S(1)}, u32[]{:S(2)}, u32[]{:S(2)}) collective-permute-start(f32[2,1,128]{2,1,0:T(1,128)S(1)} %get-tuple-element.248), channel_id=1, source_target_pairs={{0,16},{16,32},{32,48},{48,64},{64,80},{80,96},{96,112},{112,128},... | collective-permute-start | bytes 3080 | tf_op jit(solution)/shard_map/ppermute | solution.py:22
  9.0 17.4 %collective-permute-start.1 = (bf16[2,128]{1,0:T(2,128)(2,1)S(1)}, bf16[2,128]{1,0:T(2,128)(2,1)S(1)}, u32[]{:S(2)}, u32[]{:S(2)}) collective-permute-start(bf16[2,128]{1,0:T(2,128)(2,1)S(1)} %get-tuple-element.302), channel_id=1, source_target_pairs={{16,0},{32,16},{48,32},{64,48},{80,64},{96,80},{112,96},{128,112},... | collective-permute-start | bytes 1544 | tf_op jit(solution)/shard_map/ppermute | solution.py:23
  10.9 21.0 %collective-permute-start = (bf16[2,128]{1,0:T(2,128)(2,1)S(1)}, bf16[2,128]{1,0:T(2,128)(2,1)S(1)}, u32[]{:S(2)}, u32[]{:S(2)}) collective-permute-start(bf16[2,128]{1,0:T(2,128)(2,1)S(1)} %get-tuple-element.301), channel_id=1, source_target_pairs={{0,16},{16,32},{32,48},{48,64},{64,80},{80,96},{96,112},{112,128},... | collective-permute-start | bytes 1544 | tf_op jit(solution)/shard_map/ppermute | solution.py:22
  17.1 19.1 %collective-permute-start.9 = (bf16[2,128]{1,0:T(2,128)(2,1)S(1)}, bf16[2,128]{1,0:T(2,128)(2,1)S(1)}, u32[]{:S(2)}, u32[]{:S(2)}) collective-permute-start(bf16[2,128]{1,0:T(2,128)(2,1)S(1)} %get-tuple-element.300), channel_id=1, source_target_pairs={{16,0},{32,16},{48,32},{64,48},{80,64},{96,80},{112,96},{128,112},... | collective-permute-start | bytes 1544 | tf_op jit(solution)/shard_map/ppermute | solution.py:23
  19.0 0.7 copy-start.12
  19.0 6.6 copy-start.15
  26.3 24.4 %copy-start.10 = (f32[8,8,1]{1,0,2:T(8,128)}, f32[8,8,1]{1,0,2:T(8,128)S(1)}, u32[]{:S(2)}) copy-start(f32[8,8,1]{1,0,2:T(8,128)S(1)} %copy.277) | copy-start | bytes 772
  26.4 14.5 %collective-permute-start.8 = (bf16[2,128]{1,0:T(2,128)(2,1)S(1)}, bf16[2,128]{1,0:T(2,128)(2,1)S(1)}, u32[]{:S(2)}, u32[]{:S(2)}) collective-permute-start(bf16[2,128]{1,0:T(2,128)(2,1)S(1)} %get-tuple-element.299), channel_id=1, source_target_pairs={{0,16},{16,32},{32,48},{48,64},{64,80},{80,96},{96,112},{112,128},... | collective-permute-start | bytes 1544 | tf_op jit(solution)/shard_map/ppermute | solution.py:22
  32.0 11.0 %collective-permute-start.3 = (bf16[36,2]{1,0:T(8,128)(2,1)S(1)}, bf16[36,2]{1,0:T(8,128)(2,1)S(1)}, u32[]{:S(2)}, u32[]{:S(2)}) collective-permute-start(bf16[36,2]{1,0:T(8,128)(2,1)S(1)} %get-tuple-element.298), channel_id=1, source_target_pairs={{1,0},{2,1},{3,2},{4,3},{5,4},{6,5},{7,6},{8,7},{9,8},{10,9},{11,1... | collective-permute-start | bytes 440 | tf_op jit(solution)/shard_map/ppermute | solution.py:23
  36.2 11.6 %collective-permute-start.2 = (bf16[36,2]{1,0:T(8,128)(2,1)S(1)}, bf16[36,2]{1,0:T(8,128)(2,1)S(1)}, u32[]{:S(2)}, u32[]{:S(2)}) collective-permute-start(bf16[36,2]{1,0:T(8,128)(2,1)S(1)} %get-tuple-element.297), channel_id=1, source_target_pairs={{0,1},{1,2},{2,3},{3,4},{4,5},{5,6},{6,7},{7,8},{8,9},{9,10},{10,1... | collective-permute-start | bytes 440 | tf_op jit(solution)/shard_map/ppermute | solution.py:22
  41.0 12.0 %collective-permute-start.11 = (bf16[36,2]{1,0:T(8,128)(2,1)S(1)}, bf16[36,2]{1,0:T(8,128)(2,1)S(1)}, u32[]{:S(2)}, u32[]{:S(2)}) collective-permute-start(bf16[36,2]{1,0:T(8,128)(2,1)S(1)} %get-tuple-element.296), channel_id=1, source_target_pairs={{1,0},{2,1},{3,2},{4,3},{5,4},{6,5},{7,6},{8,7},{9,8},{10,9},{11,1... | collective-permute-start | bytes 440 | tf_op jit(solution)/shard_map/ppermute | solution.py:23
  42.9 15.5 %collective-permute-start.10 = (bf16[36,2]{1,0:T(8,128)(2,1)S(1)}, bf16[36,2]{1,0:T(8,128)(2,1)S(1)}, u32[]{:S(2)}, u32[]{:S(2)}) collective-permute-start(bf16[36,2]{1,0:T(8,128)(2,1)S(1)} %get-tuple-element.295), channel_id=1, source_target_pairs={{0,1},{1,2},{2,3},{3,4},{4,5},{5,6},{6,7},{7,8},{8,9},{9,10},{10,1... | collective-permute-start | bytes 440 | tf_op jit(solution)/shard_map/ppermute | solution.py:22
  51.1 11.0 %collective-permute-start.5 = (f32[8,17,128]{2,0,1:T(8,128)S(1)}, f32[8,17,128]{2,0,1:T(8,128)S(1)}, u32[]{:S(2)}, u32[]{:S(2)}) collective-permute-start(f32[8,17,128]{2,0,1:T(8,128)S(1)} %get-tuple-element.42), channel_id=1, source_target_pairs={{16,0},{32,16},{48,32},{64,48},{80,64},{96,80},{112,96},{128,112},... | collective-permute-start | bytes 208904 | tf_op jit(solution)/shard_map/ppermute | solution.py:23
  53.0 9.1 %collective-permute-start.4 = (f32[8,17,128]{2,0,1:T(8,128)S(1)}, f32[8,17,128]{2,0,1:T(8,128)S(1)}, u32[]{:S(2)}, u32[]{:S(2)}) collective-permute-start(f32[8,17,128]{2,0,1:T(8,128)S(1)} %get-tuple-element.41), channel_id=1, source_target_pairs={{0,16},{16,32},{32,48},{48,64},{64,80},{80,96},{96,112},{112,128},... | collective-permute-start | bytes 208904 | tf_op jit(solution)/shard_map/ppermute | solution.py:22
  62.0 13.0 %copy-start.18 = (f32[2,1,128]{2,1,0:T(1,128)}, f32[2,1,128]{2,1,0:T(1,128)S(1)}, u32[]{:S(2)}) copy-start(f32[2,1,128]{2,1,0:T(1,128)S(1)} %collective-permute-done.12) | copy-start | bytes 3076
  62.0 13.0 %copy-start.20 = (f32[2,1,128]{2,1,0:T(1,128)}, f32[2,1,128]{2,1,0:T(1,128)S(1)}, u32[]{:S(2)}) copy-start(f32[2,1,128]{2,1,0:T(1,128)S(1)} %collective-permute-done.13) | copy-start | bytes 3076
  62.2 12.3 %collective-permute-start.7 = (f32[8,66,17]{2,0,1:T(8,128)S(1)}, f32[8,66,17]{2,0,1:T(8,128)S(1)}, u32[]{:S(2)}, u32[]{:S(2)}) collective-permute-start(f32[8,66,17]{2,0,1:T(8,128)S(1)} %get-tuple-element.40), channel_id=1, source_target_pairs={{1,0},{2,1},{3,2},{4,3},{5,4},{6,5},{7,6},{8,7},{9,8},{10,9},{11,1... | collective-permute-start | bytes 107720 | tf_op jit(solution)/shard_map/ppermute | solution.py:23
  64.2 10.4 %collective-permute-start.6 = (f32[8,66,17]{2,0,1:T(8,128)S(1)}, f32[8,66,17]{2,0,1:T(8,128)S(1)}, u32[]{:S(2)}, u32[]{:S(2)}) collective-permute-start(f32[8,66,17]{2,0,1:T(8,128)S(1)} %get-tuple-element.39), channel_id=1, source_target_pairs={{0,1},{1,2},{2,3},{3,4},{4,5},{5,6},{6,7},{7,8},{8,9},{9,10},{10,1... | collective-permute-start | bytes 107720 | tf_op jit(solution)/shard_map/ppermute | solution.py:22
  69.7 201.3 %collective-permute-start.15 = (f32[2,34,1]{2,1,0:T(8,128)}, f32[2,34,1]{2,1,0:T(8,128)}, u32[]{:S(2)}, u32[]{:S(2)}) collective-permute-start(f32[2,34,1]{2,1,0:T(8,128)} %get-tuple-element.138), channel_id=1, source_target_pairs={{0,1},{1,2},{2,3},{3,4},{4,5},{5,6},{6,7},{7,8},{8,9},{9,10},{10,1... | collective-permute-start | bytes 824 | tf_op jit(solution)/shard_map/ppermute | solution.py:22
  71.6 199.4 %collective-permute-start.14 = (f32[2,34,1]{2,1,0:T(8,128)}, f32[2,34,1]{2,1,0:T(8,128)}, u32[]{:S(2)}, u32[]{:S(2)}) collective-permute-start(f32[2,34,1]{2,1,0:T(8,128)} %get-tuple-element.137), channel_id=1, source_target_pairs={{1,0},{2,1},{3,2},{4,3},{5,4},{6,5},{7,6},{8,7},{9,8},{10,9},{11,1... | collective-permute-start | bytes 824 | tf_op jit(solution)/shard_map/ppermute | solution.py:23
  245.6 0.7 copy-start.7
  245.7 17.5 %copy-start.11 = (pred[4096]{0:T(1024)(128)(4,1)S(1)}, pred[4096]{0:T(1024)(128)(4,1)}, u32[]{:S(2)}) copy-start(pred[4096]{0:T(1024)(128)(4,1)} %get-tuple-element.33) | copy-start | bytes 12292
  268.0 3.0 copy-start.1
  268.0 3.0 copy-start.2
  268.0 3.1 copy-start.19
  268.0 3.1 copy-start.21
  268.0 5.3 copy-start.13
  268.0 5.3 copy-start.16
  274.1 199.2 %collective-permute-start.16 = (f32[2,1,128]{2,1,0:T(1,128)}, f32[2,1,128]{2,1,0:T(1,128)S(1)}, u32[]{:S(2)}, u32[]{:S(2)}) collective-permute-start(f32[2,1,128]{2,1,0:T(1,128)} %get-tuple-element.209), channel_id=1, source_target_pairs={{16,0},{32,16},{48,32},{64,48},{80,64},{96,80},{112,96},{128,112},... | collective-permute-start | bytes 3080 | tf_op jit(solution)/shard_map/ppermute | solution.py:23
  276.0 197.3 %collective-permute-start.17 = (f32[2,1,128]{2,1,0:T(1,128)S(1)}, f32[2,1,128]{2,1,0:T(1,128)S(1)}, u32[]{:S(2)}, u32[]{:S(2)}) collective-permute-start(f32[2,1,128]{2,1,0:T(1,128)S(1)} %get-tuple-element.208), channel_id=1, source_target_pairs={{0,16},{16,32},{32,48},{48,64},{64,80},{80,96},{96,112},{112,128},... | collective-permute-start | bytes 3080 | tf_op jit(solution)/shard_map/ppermute | solution.py:22
  471.1 13.8 %copy-start.4 = (f32[2,32,128]{2,1,0:T(8,128)S(1)}, f32[2,32,128]{2,1,0:T(8,128)}, u32[]{:S(2)}) copy-start(f32[2,32,128]{2,1,0:T(8,128)} %get-tuple-element.26) | copy-start | bytes 98308
  472.7 14.2 %copy-start.14 = (s32[128]{0:T(128)S(1)}, s32[128]{0:T(128)}, u32[]{:S(2)}) copy-start(s32[128]{0:T(128)} %copy-done.12) | copy-start | bytes 1540
  472.7 14.1 %copy-start.17 = (s32[32]{0:T(128)S(1)}, s32[32]{0:T(128)}, u32[]{:S(2)}) copy-start(s32[32]{0:T(128)} %copy-done.15) | copy-start | bytes 388
  473.4 6.9 collective-permute-start.19
  478.4 6.5 collective-permute-start.18
  487.1 199.2 %collective-permute-start.20 = (f32[2,1,128]{2,1,0:T(1,128)}, f32[2,1,128]{2,1,0:T(1,128)S(1)}, u32[]{:S(2)}, u32[]{:S(2)}) collective-permute-start(f32[2,1,128]{2,1,0:T(1,128)} %get-tuple-element.179), channel_id=1, source_target_pairs={{16,0},{32,16},{48,32},{64,48},{80,64},{96,80},{112,96},{128,112},... | collective-permute-start | bytes 3080 | tf_op jit(solution)/shard_map/ppermute | solution.py:23
  489.1 197.3 %collective-permute-start.21 = (f32[2,1,128]{2,1,0:T(1,128)S(1)}, f32[2,1,128]{2,1,0:T(1,128)S(1)}, u32[]{:S(2)}, u32[]{:S(2)}) collective-permute-start(f32[2,1,128]{2,1,0:T(1,128)S(1)} %get-tuple-element.178), channel_id=1, source_target_pairs={{0,16},{16,32},{32,48},{48,64},{64,80},{80,96},{96,112},{112,128},... | collective-permute-start | bytes 3080 | tf_op jit(solution)/shard_map/ppermute | solution.py:22
  684.2 11.2 %copy-start.3 = (f32[2,32,128]{2,1,0:T(8,128)S(1)}, f32[2,32,128]{2,1,0:T(8,128)}, u32[]{:S(2)}) copy-start(f32[2,32,128]{2,1,0:T(8,128)} %param.10) | copy-start | bytes 98308
  684.2 11.2 %copy-start.5 = (f32[2,32,128]{2,1,0:T(8,128)S(1)}, f32[2,32,128]{2,1,0:T(8,128)}, u32[]{:S(2)}) copy-start(f32[2,32,128]{2,1,0:T(8,128)} %get-tuple-element.26) | copy-start | bytes 98308
  684.2 11.2 %copy-start.6 = (f32[2,32,128]{2,1,0:T(8,128)S(1)}, f32[2,32,128]{2,1,0:T(8,128)}, u32[]{:S(2)}) copy-start(f32[2,32,128]{2,1,0:T(8,128)} %get-tuple-element.17) | copy-start | bytes 98308
  686.4 4.4 collective-permute-start.23
  688.9 6.5 collective-permute-start.22
where the time goes:
time: 705 us; the launch traced here: 696 us
  local copies, waits for them, and re-layouts  481 us (68%)
  other arithmetic  115 us (16%)
  starting transfers between devices  82.8 us (12%)
  waiting for transfers between devices  9.22 us (1%)
  matrix products  7.3 us (1%)
    gather x27, local copies, waits for them, and re-layouts, sample(): jnp.take(flattened, position.reshape(-1), axis=1)  453 us
    select_n x27, other arithmetic, sample(): jnp.take(flattened, position.reshape(-1), axis=1)  97.3 us
    ppermute x12, starting transfers between devices, extended(): before = lax.ppermute(last, axis, up)  56 us
    ppermute x12, starting transfers between devices, extended(): after = lax.ppermute(leading, axis, down)  26.7 us
    reshape x27, local copies, waits for them, and re-layouts, sample(): jnp.take(flattened, position.reshape(-1), axis=1)  15.9 us
  transfers between devices with their start and end apart: 24, of which 2 were waited for; matrix products, arithmetic and copies ran while one was open for 86% of the time, Pallas kernels for 0%

commit v1 on v0

v1 whole, which is shorter than its diff:
```python
import functools

import jax
import jax.numpy as jnp
from jax import lax
from jax.experimental import pallas as pl
from jax.experimental.pallas import tpu as pltpu
from jax.sharding import PartitionSpec as P

REACH = 16
ITERS = 3
CH = 8

stiffness = 0.01
step_size = 0.5
adam_epsilon = 0.01

F32 = jnp.float32
BF16 = jnp.bfloat16
MESH = pl.DeviceIdType.MESH
AROUND = [(i, j) for i in (-1, 0, 1) for j in (-1, 0, 1) if (i, j) != (0, 0)]
SIDES = [(-1, 0), (1, 0), (0, -1), (0, 1)]
SLAB = 14


def lanes(shape):
    return lax.broadcasted_iota(jnp.int32, shape, len(shape) - 1)


def split(x):
    high = x.astype(BF16)
    return high, (x - high.astype(F32)).astype(BF16)


def dot(a, b):
    return lax.dot_general(a, b, (((1,), (0,)), ((), ())), preferred_element_type=F32)


def kernel(
    rows_of_mesh,
    cols_of_mesh,
    fixed_ref,
    moving_ref,
    field_ref,
    w1_ref,
    b1_ref,
    w2_ref,
    out_ref,
    own,
    around,
    shifted,
    toeplitz,
    lhs,
    fixed_embed,
    disp,
    edge_row,
    edge_col,
    raw,
    first_moment,
    second_moment,
    weights,
    data,
    image_send,
    image_recv,
    disp_send,
    disp_recv,
):
    me_row, me_col = lax.axis_index("row"), lax.axis_index("col")
    tile_rows, tile_cols = fixed_ref.shape

    def at(offset):
        i, j = offset
        return (
            lax.rem(me_row + (i + rows_of_mesh), rows_of_mesh),
            lax.rem(me_col + (j + cols_of_mesh), cols_of_mesh),
        )

    barrier = pltpu.get_barrier_semaphore()
    for offset in AROUND:
        pl.semaphore_signal(barrier, inc=1, device_id=at(offset), device_id_type=MESH)

    own[0] = fixed_ref[...]
    own[1] = moving_ref[...]
    raw[...] = field_ref[...]
    first_moment[...] = jnp.zeros_like(first_moment)
    second_moment[...] = jnp.zeros_like(second_moment)
    disp[0] = REACH * jnp.tanh(field_ref[...] / REACH)

    def image_copy(offset):
        i, j = offset
        slot = 3 * (1 - i) + 1 - j
        return pltpu.make_async_remote_copy(
            src_ref=own,
            dst_ref=around.at[slot],
            send_sem=image_send.at[slot],
            recv_sem=image_recv.at[slot],
            device_id=at(offset),
            device_id_type=MESH,
        )

    def disp_copy(step, side):
        i, j = SIDES[side]
        if side == 0:
            src, dst = disp.at[step, :, pl.ds(tile_rows - 8, 8), :], edge_row.at[step, 0]
        elif side == 1:
            src, dst = disp.at[step, :, pl.ds(0, 8), :], edge_row.at[step, 1]
        else:
            src, dst = disp.at[step], edge_col.at[step, side - 2]
        return pltpu.make_async_remote_copy(
            src_ref=src,
            dst_ref=dst,
            send_sem=disp_send.at[step, side],
            recv_sem=disp_recv.at[step, side],
            device_id=at((-i, -j)),
            device_id_type=MESH,
        )

    pl.semaphore_wait(barrier, len(AROUND))
    for offset in AROUND:
        image_copy(offset).start()
    for side in range(4):
        disp_copy(0, side).start()

    sub64 = lax.broadcasted_iota(jnp.int32, (64, 128), 0)
    lane64 = lanes((64, 128))
    w2 = w2_ref[...].reshape(64, 9)
    for tap_col in range(3):
        spread = jnp.zeros((64, 128), F32)
        for tap_row in range(3):
            column = w2[:, 3 * tap_row + tap_col : 3 * tap_row + tap_col + 1]
            spread = jnp.where(
                lane64 == tap_row * 8 + (sub64 & 7), jnp.broadcast_to(column, (64, 128)), spread
            )
        base = jnp.sum(spread.reshape(8, 8, 128), axis=1)
        block = jnp.concatenate(
            [base if i == 0 else pltpu.roll(base, 8 * i, 1) for i in range(SLAB)], axis=0
        )
        high, low = split(block)
        at_row = tap_col * SLAB * 8
        toeplitz[at_row : at_row + SLAB * 8, 0:128] = high
        toeplitz[at_row : at_row + SLAB * 8, 128:256] = low
    w1 = w1_ref[...]
    taps = [jnp.broadcast_to(w1[:, k : k + 1], (8, 256)) for k in range(9)]
    sub8 = lax.broadcasted_iota(jnp.int32, (8, 256), 0)
    bias = jnp.zeros((8, 256), F32)
    for ch in range(CH):
        bias = jnp.where(sub8 == ch, b1_ref[ch], bias)

    for offset in AROUND:
        image_copy(offset).wait()

    full_rows, full_cols = rows_of_mesh * tile_rows, cols_of_mesh * tile_cols
    lane_tile = lanes((80, 128))

    def encode(which, first_lane, first_row, margin, slabs, store):
        def tile(slot):
            if slot == 4:
                return own[which].astype(F32)
            row, col = me_row + (slot // 3 - 1), me_col + (slot % 3 - 1)
            inside = (row >= 0) & (row < rows_of_mesh) & (col >= 0) & (col < cols_of_mesh)
            return around[slot, which].astype(F32) * jnp.where(inside, 1.0, 0.0).astype(F32)

        bands = []
        for col in range(3):
            bands.append(
                jnp.concatenate(
                    [tile(col)[8:, :], tile(3 + col), tile(6 + col)[: tile_rows - 8, :]], axis=0
                )
            )
        for tap_col in range(3):
            start = first_lane + tap_col
            if start == 128:
                left, right = bands[1], bands[2]
            else:
                turned = [pltpu.roll(x, 128 - start, 1) for x in bands]
                inside = lane_tile < 128 - start
                left = jnp.where(inside, turned[0], turned[1])
                right = jnp.where(inside, turned[1], turned[2])
            shifted[tap_col, :, 0:128] = left
            shifted[tap_col, :, 128:256] = right

        lane8 = lanes((8, 256))
        col8 = me_col * tile_cols + lane8 - (margin + 1)
        col_in = (col8 >= 0) & (col8 < full_cols)
        lane_e = lanes((SLAB * 8, 256))
        row_e = lax.broadcasted_iota(jnp.int32, (SLAB * 8, 256), 0) // 8
        col_e = me_col * tile_cols + lane_e - margin
        ok_col = (col_e >= 0) & (col_e < full_cols) & (lane_e < tile_cols + 2 * margin)

        for slab in slabs:
            hidden = []
            for i in range(SLAB + 2):
                h = bias
                for tap in range(9):
                    pixel = shifted[tap % 3, pl.ds(first_row + slab + i + tap // 3, 1), :]
                    h = h + taps[tap] * jnp.broadcast_to(pixel, (8, 256))
                row = me_row * tile_rows + (slab + i - margin - 1)
                row_ok = (row >= 0) & (row < full_rows)
                row_factor = jnp.where(row_ok, 1.0, 0.0).astype(F32)
                hidden.append(jnp.where(col_in, jnp.maximum(h, 0.0) * row_factor, 0.0))
            high, low = split(jnp.concatenate(hidden, axis=0))
            t_high, t_low = toeplitz[:, 0:128], toeplitz[:, 128:256]
            product = dot(
                jnp.concatenate([t_high, t_high], axis=1), jnp.concatenate([high, low], axis=0)
            ) + dot(t_low, high)
            n = SLAB * 8
            embed = (
                product[0:n]
                + pltpu.roll(product[n : 2 * n], 255, 1)
                + pltpu.roll(product[2 * n : 3 * n], 254, 1)
            )
            row_abs = me_row * tile_rows + row_e + (slab - margin)
            embed = jnp.where(ok_col & (row_abs >= 0) & (row_abs < full_rows), embed, 0.0)
            store(slab, embed)

    def halves(even, odd, low_half):
        axis = even.ndim - 1
        return (
            jnp.where(low_half, even, pltpu.roll(odd, 64, axis)),
            jnp.where(low_half, pltpu.roll(even, 64, axis), odd),
        )

    low8 = lanes((8, 128)) < 64

    def store_fixed(slab, embed):
        for pair in range(SLAB // 2):
            even = embed[pair * 16 : pair * 16 + 8, 0:128]
            odd = embed[pair * 16 + 8 : pair * 16 + 16, 0:128]
            left, right = halves(even, odd, low8)
            fixed_embed[slab // 2 + pair] = left
            fixed_embed[16 + slab // 2 + pair] = right

    low_e = lanes((SLAB * 8, 128)) < 64

    def store_moving(slab, embed):
        a, b = embed[:, 0:128], embed[:, 128:256]
        middle = jnp.where(low_e, pltpu.roll(a, 64, 1), pltpu.roll(b, 64, 1))
        for half, part in enumerate((a, middle)):
            high, low = split(part)
            lhs[half, slab * 8 : (slab + SLAB) * 8, 0:128] = high
            lhs[half, slab * 8 : (slab + SLAB) * 8, 128:256] = low

    encode(0, 126, 22, 0, (0, 14, 18), store_fixed)
    encode(1, 109, 5, REACH + 1, (0, 14, 28, 42, 52), store_moving)

    low16 = lanes((16, 128)) < 64
    lane32 = lanes((32, 128))
    position = (lane32 & 63).astype(F32) + (REACH + 1)
    second_row = jnp.where(lane32 >= 64, 1.0, 0.0).astype(F32)
    row32 = lax.broadcasted_iota(jnp.int32, (tile_rows, tile_cols), 0)
    has_north = jnp.where(me_row > 0, 1.0, 0.0).astype(F32)
    has_south = jnp.where(me_row < rows_of_mesh - 1, 1.0, 0.0).astype(F32)
    has_west = jnp.where(me_col > 0, 1.0, 0.0).astype(F32)
    has_east = jnp.where(me_col < cols_of_mesh - 1, 1.0, 0.0).astype(F32)

    def step(it, carry):
        grouped = []
        for comp in range(2):
            even = disp[it, comp, pl.ds(0, 16, stride=2), :]
            odd = disp[it, comp, pl.ds(1, 16, stride=2), :]
            grouped.append(jnp.concatenate(halves(even, odd, low16), axis=0))
        for comp in range(2):
            nearest = jnp.floor(grouped[comp] + 0.5)
            f = grouped[comp] - nearest
            at_w = 6 * comp
            weights[at_w] = 0.5 * (0.5 - f) * (0.5 - f)
            weights[at_w + 1] = 0.75 - f * f
            weights[at_w + 2] = 0.5 * (0.5 + f) * (0.5 + f)
            weights[at_w + 3] = f - 0.5
            weights[at_w + 4] = -2.0 * f
            weights[at_w + 5] = 0.5 + f
            if comp == 0:
                weights[12] = nearest + REACH + second_row
            else:
                weights[13] = nearest + position

        place = lax.broadcasted_iota(jnp.int32, (128, 128), 0).astype(F32)

        def sample(index, carry):
            half = index // 8
            quad = lax.rem(index, 8)
            columns = []
            for j in range(2):
                group = half * 16 + quad * 2 + j
                target = jnp.broadcast_to(weights[13, pl.ds(group, 1), :], (128, 128))
                off = place - target
                for b in range(3):
                    columns.append(jnp.where(off == b - 1, 1.0, 0.0).astype(BF16))
            onehot = jnp.concatenate(columns, axis=1)
            window = lhs[half, pl.ds(pl.multiple_of(quad * 32, 32), 304), :]
            picked = dot(window, jnp.concatenate([onehot, onehot], axis=0))
            for j in range(2):
                group = half * 16 + quad * 2 + j

                def weight(k):
                    return jnp.broadcast_to(weights[k, pl.ds(group, 1), :], (8, 128))

                offset = weight(12)
                masks = []
                for shift in (17, 8, 4, 2, 1, 1):
                    mask = offset >= shift
                    masks.append(mask)
                    offset = jnp.where(mask, offset - shift, offset)
                taps_at = []
                for b in range(3):
                    n = 3 * j + b
                    rows = [
                        picked[(2 * j + k) * 8 : (2 * j + k) * 8 + 8, n * 128 : n * 128 + 128]
                        for k in range(36)
                    ]
                    for shift, mask, count in zip(
                        (17, 8, 4, 2, 1, 1), masks, (19, 11, 7, 5, 4, 3)
                    ):
                        rows = [jnp.where(mask, rows[k + shift], rows[k]) for k in range(count)]
                    taps_at.append(rows)
                warped = slope_row = slope_col = None
                for b in range(3):
                    along = sum(weight(a) * taps_at[b][a] for a in range(3))
                    slant = sum(weight(3 + a) * taps_at[b][a] for a in range(3))
                    w, dw = weight(6 + b), weight(9 + b)
                    terms = (w * along, w * slant, dw * along)
                    if b == 0:
                        warped, slope_row, slope_col = terms
                    else:
                        warped += terms[0]
                        slope_row += terms[1]
                        slope_col += terms[2]
                mismatch = warped - fixed_embed[group]
                data[0, pl.ds(group, 1), :] = jnp.sum(mismatch * slope_row, axis=0, keepdims=True)
                data[1, pl.ds(group, 1), :] = jnp.sum(mismatch * slope_col, axis=0, keepdims=True)
            return carry

        lax.fori_loop(0, 16, sample, 0)

        for side in range(4):
            disp_copy(it, side).wait_recv()
        lane = lanes((tile_rows, tile_cols))
        one = jnp.where(it == 0, 1 / (1 - 0.9), jnp.where(it == 1, 1 / (1 - 0.9**2), 1 / (1 - 0.9**3)))
        two = jnp.where(
            it == 0, 1 / (1 - 0.999), jnp.where(it == 1, 1 / (1 - 0.999**2), 1 / (1 - 0.999**3))
        )
        for comp in range(2):
            even, odd = halves(data[comp, 0:16, :], data[comp, 16:32, :], low16)
            out_ref[comp, pl.ds(0, 16, stride=2), :] = even
            out_ref[comp, pl.ds(1, 16, stride=2), :] = odd
            sampled = out_ref[comp] * (2.0 / CH)
            d = disp[it, comp]
            north = jnp.where(
                row32 == 0, has_north * edge_row[it, 0, comp, 7:8, :], pltpu.roll(d, 1, 0)
            )
            south = jnp.where(
                row32 == tile_rows - 1,
                has_south * edge_row[it, 1, comp, 0:1, :],
                pltpu.roll(d, tile_rows - 1, 0),
            )
            west = pltpu.roll(
                jnp.where(lane == tile_cols - 1, has_west * edge_col[it, 0, comp], d), 1, 1
            )
            east = pltpu.roll(
                jnp.where(lane == 0, has_east * edge_col[it, 1, comp], d), tile_cols - 1, 1
            )
            squashed = d * (1.0 / REACH)
            gradient = (
                sampled + 2.0 * stiffness * (4.0 * d - (south + north + east + west))
            ) * (1.0 - squashed * squashed)
            m1 = 0.9 * first_moment[comp] + 0.1 * gradient
            m2 = 0.999 * second_moment[comp] + 0.001 * gradient * gradient
            first_moment[comp] = m1
            second_moment[comp] = m2
            new = raw[comp] - step_size * (m1 * one) / (jnp.sqrt(m2 * two) + adam_epsilon)
            raw[comp] = new

            @pl.when(it < ITERS - 1)
            def _():
                disp[it + 1, comp] = REACH * jnp.tanh(new / REACH)

        @pl.when(it < ITERS - 1)
        def _():
            for side in range(4):
                disp_copy(it + 1, side).start()

        return carry

    lax.fori_loop(0, ITERS, step, 0)
    out_ref[...] = raw[...] - field_ref[...]
    for it in range(ITERS):
        for side in range(4):
            disp_copy(it, side).wait_send()


def local(rows_of_mesh, cols_of_mesh, fixed, moving, field, w1, b1, w2):
    tile_rows, tile_cols = fixed.shape
    vmem = pl.BlockSpec(memory_space=pltpu.VMEM)
    tile = (tile_rows, tile_cols)
    return pl.pallas_call(
        functools.partial(kernel, rows_of_mesh, cols_of_mesh),
        out_shape=jax.ShapeDtypeStruct(field.shape, F32),
        in_specs=[vmem, vmem, vmem, vmem, pl.BlockSpec(memory_space=pltpu.SMEM), vmem],
        out_specs=vmem,
        scratch_shapes=[
            pltpu.VMEM((2,) + tile, BF16),
            pltpu.VMEM((9, 2) + tile, BF16),
            pltpu.VMEM((3, 80, 256), F32),
            pltpu.VMEM((3 * SLAB * 8, 256), BF16),
            pltpu.VMEM((2, 66 * 8, 256), BF16),
            pltpu.VMEM((32, 8, 128), F32),
            pltpu.VMEM((ITERS, 2) + tile, F32),
            pltpu.VMEM((ITERS, 2, 2, 8, tile_cols), F32),
            pltpu.VMEM((ITERS, 2, 2) + tile, F32),
            pltpu.VMEM((2,) + tile, F32),
            pltpu.VMEM((2,) + tile, F32),
            pltpu.VMEM((2,) + tile, F32),
            pltpu.VMEM((14, 32, 128), F32),
            pltpu.VMEM((2, 32, 128), F32),
            pltpu.SemaphoreType.DMA((9,)),
            pltpu.SemaphoreType.DMA((9,)),
            pltpu.SemaphoreType.DMA((ITERS, 4)),
            pltpu.SemaphoreType.DMA((ITERS, 4)),
        ],
        compiler_params=pltpu.CompilerParams(
            collective_id=0, has_side_effects=True, vmem_limit_bytes=40 << 20
        ),
        name="refine",
    )(fixed, moving, field, w1, b1, w2)


def solution(mesh):
    return jax.shard_map(
        functools.partial(local, mesh.shape["row"], mesh.shape["col"]),
        mesh=mesh,
        in_specs=(P("row", "col"), P("row", "col"), P(None, "row", "col"), P(), P(), P()),
        out_specs=P(None, "row", "col"),
        check_vma=False,
    )
```

time: 705 us -> 38.1 us (0.05)
  the two profiles are of different devices: /device:TPU:121 before, /device:TPU:1 now
where the time goes in v1:
time: 38.1 us; the launch traced here: 37.8 us
  Pallas kernels  32.9 us (86%)
  local copies, waits for them, and re-layouts  4.87 us (13%)
    pallas_call x1, Pallas kernels, local(): pl.pallas_call(functools.partial(kernel, rows_of_mesh, cols_of_mesh), out...  32.9 us
    unnamed x13, local copies, waits for them, and re-layouts  4.87 us

profile of v1, /device:TPU:1, one launch (start us, length us, event | category | flops | bytes accessed | tf_op | source)
XLA Modules:
  0.0 37.8 jit_solution(3096188781160662362)
XLA Ops:
  0.0 0.0 copy-start
  0.0 0.8 %copy-done = f32[2,32,128]{2,1,0:T(8,128)S(1)} copy-done((f32[2,32,128]{2,1,0:T(8,128)S(1)}, f32[2,32,128]{2,1,0:T(8,128)}, u32[]{:S(2)}) %copy-start) | copy-done | bytes 32792
  0.8 0.0 copy-start.1
  0.8 0.8 %copy-done.1 = f32[8,8,9]{2,1,0:T(8,128)S(1)} copy-done((f32[8,8,9]{2,1,0:T(8,128)S(1)}, f32[8,8,9]{2,1,0:T(8,128)}, u32[]{:S(2)}) %copy-start.1) | copy-done | bytes 2328
  1.5 0.0 copy-start.2
  1.5 0.7 %copy-done.2 = bf16[32,128]{1,0:T(8,128)(2,1)S(1)} copy-done((bf16[32,128]{1,0:T(8,128)(2,1)S(1)}, bf16[32,128]{1,0:T(8,128)(2,1)}, u32[]{:S(2)}) %copy-start.2) | copy-done | bytes 8216
  2.2 0.0 copy-start.3
  2.2 0.7 %copy-done.3 = bf16[32,128]{1,0:T(8,128)(2,1)S(1)} copy-done((bf16[32,128]{1,0:T(8,128)(2,1)S(1)}, bf16[32,128]{1,0:T(8,128)(2,1)}, u32[]{:S(2)}) %copy-start.3) | copy-done | bytes 8216
  2.9 0.0 copy-start.4
  2.9 0.7 %copy-done.4 = f32[8,9]{1,0:T(8,128)S(1)} copy-done((f32[8,9]{1,0:T(8,128)S(1)}, f32[8,9]{1,0:T(8,128)}, u32[]{:S(2)}) %copy-start.4) | copy-done | bytes 312
  3.6 0.0 copy-start.5
  3.6 0.7 %copy-done.5 = f32[8]{0:T(128)S(1)} copy-done((f32[8]{0:T(128)S(1)}, f32[8]{0:T(128)}, u32[]{:S(2)}) %copy-start.5) | copy-done | bytes 56
  4.3 32.9 %refine.1 = f32[2,32,128]{2,1,0:T(8,128)S(1)} custom-call(bf16[32,128]{1,0:T(8,128)(2,1)S(1)} %copy-done.2, bf16[32,128]{1,0:T(8,128)(2,1)S(1)} %copy-done.3, f32[2,32,128]{2,1,0:T(8,128)S(1)} %copy-done, f32[8,9]{1,0:T(8,128)S(1)} %copy-done.4, f32[8]{0:T(128)S(1)} %copy-done.5, f32[8,8,9]{2,1,0:T(8,128)S(1)} %copy-done.1), custom_call_target="tpu_custom_call" | custom-call | tf_op jit(solution)/shard_map/refine/pallas_call | solution.py:395
  37.1 0.6 %copy.8 = f32[2,32,128]{2,1,0:T(8,128)} copy(f32[2,32,128]{2,1,0:T(8,128)S(1)} %refine.1) | data formatting | bytes 65536
Async XLA Ops:
  0.0 0.8 %copy-start = (f32[2,32,128]{2,1,0:T(8,128)S(1)}, f32[2,32,128]{2,1,0:T(8,128)}, u32[]{:S(2)}) copy-start(f32[2,32,128]{2,1,0:T(8,128)} %field_ref.1) | copy-start | bytes 98308
  0.8 0.8 %copy-start.1 = (f32[8,8,9]{2,1,0:T(8,128)S(1)}, f32[8,8,9]{2,1,0:T(8,128)}, u32[]{:S(2)}) copy-start(f32[8,8,9]{2,1,0:T(8,128)} %w2_ref.1) | copy-start | bytes 6916
  1.5 0.7 %copy-start.2 = (bf16[32,128]{1,0:T(8,128)(2,1)S(1)}, bf16[32,128]{1,0:T(8,128)(2,1)}, u32[]{:S(2)}) copy-start(bf16[32,128]{1,0:T(8,128)(2,1)} %fixed_ref.1) | copy-start | bytes 24580
  2.2 0.7 %copy-start.3 = (bf16[32,128]{1,0:T(8,128)(2,1)S(1)}, bf16[32,128]{1,0:T(8,128)(2,1)}, u32[]{:S(2)}) copy-start(bf16[32,128]{1,0:T(8,128)(2,1)} %moving_ref.1) | copy-start | bytes 24580
  2.9 0.7 %copy-start.4 = (f32[8,9]{1,0:T(8,128)S(1)}, f32[8,9]{1,0:T(8,128)}, u32[]{:S(2)}) copy-start(f32[8,9]{1,0:T(8,128)} %w1_ref.1) | copy-start | bytes 868
  3.6 0.7 %copy-start.5 = (f32[8]{0:T(128)S(1)}, f32[8]{0:T(128)}, u32[]{:S(2)}) copy-start(f32[8]{0:T(128)} %b1_ref.1) | copy-start | bytes 100

commit v2 on v1

--- a/solution.py
+++ b/solution.py
@@ -39,13 +39,17 @@
 def kernel(
     rows_of_mesh,
     cols_of_mesh,
-    fixed_ref,
-    moving_ref,
+    fixed_hbm,
+    moving_hbm,
+    field_hbm,
+    w1_hbm,
+    b1_hbm,
+    w2_hbm,
+    out_ref,
     field_ref,
     w1_ref,
     b1_ref,
     w2_ref,
-    out_ref,
     own,
     around,
     shifted,
@@ -64,9 +68,10 @@
     image_recv,
     disp_send,
     disp_recv,
+    load_sem,
 ):
     me_row, me_col = lax.axis_index("row"), lax.axis_index("col")
-    tile_rows, tile_cols = fixed_ref.shape
+    tile_rows, tile_cols = fixed_hbm.shape
 
     def at(offset):
         i, j = offset
@@ -79,12 +84,28 @@
     for offset in AROUND:
         pl.semaphore_signal(barrier, inc=1, device_id=at(offset), device_id_type=MESH)
 
-    own[0] = fixed_ref[...]
-    own[1] = moving_ref[...]
-    raw[...] = field_ref[...]
+    loads = [
+        pltpu.make_async_copy(src, dst, load_sem.at[i])
+        for i, (src, dst) in enumerate(
+            [
+                (field_hbm, field_ref),
+                (moving_hbm, own.at[1]),
+                (fixed_hbm, own.at[0]),
+                (w2_hbm, w2_ref),
+                (w1_hbm, w1_ref),
+                (b1_hbm, b1_ref),
+            ]
+        )
+    ]
+    for load in loads:
+        load.start()
     first_moment[...] = jnp.zeros_like(first_moment)
     second_moment[...] = jnp.zeros_like(second_moment)
+    loads[0].wait()
+    raw[...] = field_ref[...]
     disp[0] = REACH * jnp.tanh(field_ref[...] / REACH)
+    for load in loads[1:]:
+        load.wait()
 
     def image_copy(offset):
         i, j = offset
@@ -330,7 +351,7 @@
                 data[1, pl.ds(group, 1), :] = jnp.sum(mismatch * slope_col, axis=0, keepdims=True)
             return carry
 
-        lax.fori_loop(0, 16, sample, 0)
+        lax.fori_loop(0, 16, sample, 0, unroll=8)
 
         for side in range(4):
             disp_copy(it, side).wait_recv()
@@ -395,9 +416,13 @@
     return pl.pallas_call(
         functools.partial(kernel, rows_of_mesh, cols_of_mesh),
         out_shape=jax.ShapeDtypeStruct(field.shape, F32),
-        in_specs=[vmem, vmem, vmem, vmem, pl.BlockSpec(memory_space=pltpu.SMEM), vmem],
+        in_specs=[pl.BlockSpec(memory_space=pltpu.HBM)] * 6,
         out_specs=vmem,
         scratch_shapes=[
+            pltpu.VMEM(field.shape, F32),
+            pltpu.VMEM(w1.shape, F32),
+            pltpu.SMEM(b1.shape, F32),
+            pltpu.VMEM(w2.shape, F32),
             pltpu.VMEM((2,) + tile, BF16),
             pltpu.VMEM((9, 2) + tile, BF16),
             pltpu.VMEM((3, 80, 256), F32),
@@ -416,9 +441,10 @@
             pltpu.SemaphoreType.DMA((9,)),
             pltpu.SemaphoreType.DMA((ITERS, 4)),
             pltpu.SemaphoreType.DMA((ITERS, 4)),
+            pltpu.SemaphoreType.DMA((6,)),
         ],
         compiler_params=pltpu.CompilerParams(
-            collective_id=0, has_side_effects=True, vmem_limit_bytes=40 << 20
+            collective_id=0, has_side_effects=True, vmem_limit_bytes=60 << 20
         ),
         name="refine",
     )(fixed, moving, field, w1, b1, w2)

time: 38.1 us -> 30 us (0.79)
  Pallas kernels: 32.9 us -> 28.4 us
  local copies, waits for them, and re-layouts: 4.87 us -> 1.38 us
    pallas_call x1, Pallas kernels: 32.9 us -> 28.4 us  [local(): pl.pallas_call(functools.partial(kernel, rows_of_mesh, cols_of_mesh), out...]
    unnamed x13 -> x1, local copies, waits for them, and re-layouts: 4.87 us -> 1.38 us
where the time goes in v2:
time: 30 us; the launch traced here: 29.8 us
  Pallas kernels  28.4 us (95%)
  local copies, waits for them, and re-layouts  1.38 us (5%)
    pallas_call x1, Pallas kernels, local(): pl.pallas_call(functools.partial(kernel, rows_of_mesh, cols_of_mesh), out...  28.4 us
    unnamed x1, local copies, waits for them, and re-layouts  1.38 us

profile of v2, /device:TPU:1, one launch (start us, length us, event | category | flops | bytes accessed | tf_op | source)
XLA Modules:
  0.0 29.8 jit_solution(11267479138414779872)
XLA Ops:
  0.0 28.4 %refine.1 = f32[2,32,128]{2,1,0:T(8,128)} custom-call(bf16[32,128]{1,0:T(8,128)(2,1)} %fixed_hbm.1, bf16[32,128]{1,0:T(8,128)(2,1)} %moving_hbm.1, f32[2,32,128]{2,1,0:T(8,128)} %field_hbm.1, f32[8,9]{1,0:T(8,128)} %w1_hbm.1, f32[8]{0:T(128)} %b1_hbm.1, f32[8,8,9]{2,1,0:T(8,128)} %w2_hbm.1), custom_call_target="tpu_custom_call" | custom-call | tf_op jit(solution)/shard_map/refine/pallas_call | solution.py:416
  28.4 1.4 %copy.8 = f32[2,32,128]{2,1,0:T(8,128)} copy(f32[2,32,128]{2,1,0:T(8,128)} %refine.1) | data formatting | bytes 65536

commit v3 on v2

--- a/solution.py
+++ b/solution.py
@@ -74,15 +74,18 @@
     tile_rows, tile_cols = fixed_hbm.shape
 
     def at(offset):
-        i, j = offset
-        return (
-            lax.rem(me_row + (i + rows_of_mesh), rows_of_mesh),
-            lax.rem(me_col + (j + cols_of_mesh), cols_of_mesh),
-        )
+        return me_row + offset[0], me_col + offset[1]
+
+    def present(offset):
+        row, col = at(offset)
+        return (row >= 0) & (row < rows_of_mesh) & (col >= 0) & (col < cols_of_mesh)
 
     barrier = pltpu.get_barrier_semaphore()
     for offset in AROUND:
-        pl.semaphore_signal(barrier, inc=1, device_id=at(offset), device_id_type=MESH)
+
+        @pl.when(present(offset))
+        def _():
+            pl.semaphore_signal(barrier, inc=1, device_id=at(offset), device_id_type=MESH)
 
     loads = [
         pltpu.make_async_copy(src, dst, load_sem.at[i])
@@ -99,6 +102,22 @@
     ]
     for load in loads:
         load.start()
+    for offset in AROUND:
+        slot = 3 * (offset[0] + 1) + offset[1] + 1
+
+        @pl.when(jnp.logical_not(present(offset)))
+        def _():
+            around[slot] = jnp.zeros(around.shape[1:], BF16)
+
+    for side in range(4):
+
+        @pl.when(jnp.logical_not(present(SIDES[side])))
+        def _():
+            if side < 2:
+                edge_row[:, side] = jnp.zeros((ITERS,) + edge_row.shape[2:], F32)
+            else:
+                edge_col[:, side - 2] = jnp.zeros((ITERS,) + edge_col.shape[2:], F32)
+
     first_moment[...] = jnp.zeros_like(first_moment)
     second_moment[...] = jnp.zeros_like(second_moment)
     loads[0].wait()
@@ -107,15 +126,14 @@
     for load in loads[1:]:
         load.wait()
 
-    def image_copy(offset):
-        i, j = offset
-        slot = 3 * (1 - i) + 1 - j
+    def image_copy(slot):
+        i, j = 1 - slot // 3, 1 - slot % 3
         return pltpu.make_async_remote_copy(
             src_ref=own,
             dst_ref=around.at[slot],
             send_sem=image_send.at[slot],
             recv_sem=image_recv.at[slot],
-            device_id=at(offset),
+            device_id=at((i, j)),
             device_id_type=MESH,
         )
 
@@ -136,11 +154,24 @@
             device_id_type=MESH,
         )
 
-    pl.semaphore_wait(barrier, len(AROUND))
-    for offset in AROUND:
-        image_copy(offset).start()
-    for side in range(4):
-        disp_copy(0, side).start()
+    def send_disp(step):
+        for side in range(4):
+            i, j = SIDES[side]
+
+            @pl.when(present((-i, -j)))
+            def _():
+                disp_copy(step, side).start()
+
+    rows_near = 1 + (me_row > 0).astype(jnp.int32) + (me_row < rows_of_mesh - 1).astype(jnp.int32)
+    cols_near = 1 + (me_col > 0).astype(jnp.int32) + (me_col < cols_of_mesh - 1).astype(jnp.int32)
+    pl.semaphore_wait(barrier, rows_near * cols_near - 1)
+    for i, j in AROUND:
+
+        @pl.when(present((-i, -j)))
+        def _():
+            image_copy(3 * (i + 1) + j + 1).start()
+
+    send_disp(0)
 
     sub64 = lax.broadcasted_iota(jnp.int32, (64, 128), 0)
     lane64 = lanes((64, 128))
@@ -167,8 +198,11 @@
     for ch in range(CH):
         bias = jnp.where(sub8 == ch, b1_ref[ch], bias)
 
-    for offset in AROUND:
-        image_copy(offset).wait()
+    for i, j in AROUND:
+
+        @pl.when(present((i, j)))
+        def _():
+            image_copy(3 * (i + 1) + j + 1).wait_recv()
 
     full_rows, full_cols = rows_of_mesh * tile_rows, cols_of_mesh * tile_cols
     lane_tile = lanes((80, 128))
@@ -177,9 +211,7 @@
         def tile(slot):
             if slot == 4:
                 return own[which].astype(F32)
-            row, col = me_row + (slot // 3 - 1), me_col + (slot % 3 - 1)
-            inside = (row >= 0) & (row < rows_of_mesh) & (col >= 0) & (col < cols_of_mesh)
-            return around[slot, which].astype(F32) * jnp.where(inside, 1.0, 0.0).astype(F32)
+            return around[slot, which].astype(F32)
 
         bands = []
         for col in range(3):
@@ -269,10 +301,6 @@
     position = (lane32 & 63).astype(F32) + (REACH + 1)
     second_row = jnp.where(lane32 >= 64, 1.0, 0.0).astype(F32)
     row32 = lax.broadcasted_iota(jnp.int32, (tile_rows, tile_cols), 0)
-    has_north = jnp.where(me_row > 0, 1.0, 0.0).astype(F32)
-    has_south = jnp.where(me_row < rows_of_mesh - 1, 1.0, 0.0).astype(F32)
-    has_west = jnp.where(me_col > 0, 1.0, 0.0).astype(F32)
-    has_east = jnp.where(me_col < cols_of_mesh - 1, 1.0, 0.0).astype(F32)
 
     def step(it, carry):
         grouped = []
@@ -354,7 +382,11 @@
         lax.fori_loop(0, 16, sample, 0, unroll=8)
 
         for side in range(4):
-            disp_copy(it, side).wait_recv()
+
+            @pl.when(present(SIDES[side]))
+            def _():
+                disp_copy(it, side).wait_recv()
+
         lane = lanes((tile_rows, tile_cols))
         one = jnp.where(it == 0, 1 / (1 - 0.9), jnp.where(it == 1, 1 / (1 - 0.9**2), 1 / (1 - 0.9**3)))
         two = jnp.where(
@@ -367,18 +399,18 @@
             sampled = out_ref[comp] * (2.0 / CH)
             d = disp[it, comp]
             north = jnp.where(
-                row32 == 0, has_north * edge_row[it, 0, comp, 7:8, :], pltpu.roll(d, 1, 0)
+                row32 == 0, edge_row[it, 0, comp, 7:8, :], pltpu.roll(d, 1, 0)
             )
             south = jnp.where(
                 row32 == tile_rows - 1,
-                has_south * edge_row[it, 1, comp, 0:1, :],
+                edge_row[it, 1, comp, 0:1, :],
                 pltpu.roll(d, tile_rows - 1, 0),
             )
             west = pltpu.roll(
-                jnp.where(lane == tile_cols - 1, has_west * edge_col[it, 0, comp], d), 1, 1
+                jnp.where(lane == tile_cols - 1, edge_col[it, 0, comp], d), 1, 1
             )
             east = pltpu.roll(
-                jnp.where(lane == 0, has_east * edge_col[it, 1, comp], d), tile_cols - 1, 1
+                jnp.where(lane == 0, edge_col[it, 1, comp], d), tile_cols - 1, 1
             )
             squashed = d * (1.0 / REACH)
             gradient = (
@@ -397,16 +429,25 @@
 
         @pl.when(it < ITERS - 1)
         def _():
-            for side in range(4):
-                disp_copy(it + 1, side).start()
+            send_disp(it + 1)
 
         return carry
 
     lax.fori_loop(0, ITERS, step, 0)
     out_ref[...] = raw[...] - field_ref[...]
-    for it in range(ITERS):
-        for side in range(4):
-            disp_copy(it, side).wait_send()
+    for i, j in AROUND:
+
+        @pl.when(present((-i, -j)))
+        def _():
+            image_copy(3 * (i + 1) + j + 1).wait_send()
+
+    for side in range(4):
+        i, j = SIDES[side]
+
+        @pl.when(present((-i, -j)))
+        def _():
+            for it in range(ITERS):
+                disp_copy(it, side).wait_send()
 
 
 def local(rows_of_mesh, cols_of_mesh, fixed, moving, field, w1, b1, w2):

time: 30 us -> 25.7 us (0.86)
  the two profiles are of different devices: /device:TPU:1 before, /device:TPU:103 now
where the time goes in v3:
time: 25.7 us; the launch traced here: 25.5 us
  Pallas kernels  24.1 us (94%)
  local copies, waits for them, and re-layouts  1.38 us (5%)
    pallas_call x1, Pallas kernels, local(): pl.pallas_call(functools.partial(kernel, rows_of_mesh, cols_of_mesh), out...  24.1 us
    unnamed x1, local copies, waits for them, and re-layouts  1.38 us

profile of v3, /device:TPU:103, one launch (start us, length us, event | category | flops | bytes accessed | tf_op | source)
XLA Modules:
  0.0 25.5 jit_solution(9478625201861893245)
XLA Ops:
  0.0 24.1 %refine.1 = f32[2,32,128]{2,1,0:T(8,128)} custom-call(bf16[32,128]{1,0:T(8,128)(2,1)} %fixed_hbm.1, bf16[32,128]{1,0:T(8,128)(2,1)} %moving_hbm.1, f32[2,32,128]{2,1,0:T(8,128)} %field_hbm.1, f32[8,9]{1,0:T(8,128)} %w1_hbm.1, f32[8]{0:T(128)} %b1_hbm.1, f32[8,8,9]{2,1,0:T(8,128)} %w2_hbm.1), custom_call_target="tpu_custom_call" | custom-call | tf_op jit(solution)/shard_map/refine/pallas_call | solution.py:457
  24.1 1.4 %copy.8 = f32[2,32,128]{2,1,0:T(8,128)} copy(f32[2,32,128]{2,1,0:T(8,128)} %refine.1) | data formatting | bytes 65536

commit v4 on v3

v4 whole, which is shorter than its diff:
```python
import functools

import jax
import jax.numpy as jnp
from jax import lax
from jax.experimental import pallas as pl
from jax.experimental.pallas import tpu as pltpu
from jax.sharding import PartitionSpec as P

REACH = 16
ITERS = 3
CH = 8

stiffness = 0.01
step_size = 0.5
adam_epsilon = 0.01

F32 = jnp.float32
BF16 = jnp.bfloat16
MESH = pl.DeviceIdType.MESH
AROUND = [(i, j) for i in (-1, 0, 1) for j in (-1, 0, 1) if (i, j) != (0, 0)]
NORTH_SOUTH = [(-1, 0), (1, 0)]
WEST_EAST = [(0, -1), (0, 1)]
HALO = 8
EXTRA = 2
SLAB = 14


def lanes(shape):
    return lax.broadcasted_iota(jnp.int32, shape, len(shape) - 1)


def split(x):
    high = x.astype(BF16)
    return high, (x - high.astype(F32)).astype(BF16)


def dot(a, b):
    return lax.dot_general(a, b, (((1,), (0,)), ((), ())), preferred_element_type=F32)


def kernel(
    rows_of_mesh,
    cols_of_mesh,
    fixed_hbm,
    moving_hbm,
    field_hbm,
    w1_hbm,
    b1_hbm,
    w2_hbm,
    out_ref,
    field_ref,
    w1_ref,
    b1_ref,
    w2_ref,
    own,
    around,
    shifted,
    toeplitz,
    lhs,
    lhs_f32,
    fixed_embed,
    disp,
    edge_col,
    raw,
    first_moment,
    second_moment,
    weights,
    data,
    unpaired,
    image_send,
    image_recv,
    field_send,
    field_recv,
    disp_send,
    disp_recv,
    load_sem,
):
    me_row, me_col = lax.axis_index("row"), lax.axis_index("col")
    tile_rows, tile_cols = fixed_hbm.shape
    ext_rows = tile_rows + 2 * HALO

    def at(offset):
        return me_row + offset[0], me_col + offset[1]

    def present(offset):
        row, col = at(offset)
        return (row >= 0) & (row < rows_of_mesh) & (col >= 0) & (col < cols_of_mesh)

    barrier = pltpu.get_barrier_semaphore()
    for offset in AROUND:

        @pl.when(present(offset))
        def _():
            pl.semaphore_signal(barrier, inc=1, device_id=at(offset), device_id_type=MESH)

    loads = [
        pltpu.make_async_copy(src, dst, load_sem.at[i])
        for i, (src, dst) in enumerate(
            [
                (field_hbm, field_ref.at[:, pl.ds(HALO, tile_rows), :]),
                (moving_hbm, own.at[1]),
                (fixed_hbm, own.at[0]),
                (w2_hbm, w2_ref),
                (w1_hbm, w1_ref),
                (b1_hbm, b1_ref),
            ]
        )
    ]
    for load in loads:
        load.start()
    for offset in AROUND:
        slot = 3 * (offset[0] + 1) + offset[1] + 1

        @pl.when(jnp.logical_not(present(offset)))
        def _():
            around[slot] = jnp.zeros(around.shape[1:], BF16)

    for side in range(2):

        @pl.when(jnp.logical_not(present(NORTH_SOUTH[side])))
        def _():
            at_row = side * (HALO + tile_rows)
            field_ref[:, at_row : at_row + HALO, :] = jnp.zeros((2, HALO, tile_cols), F32)

        @pl.when(jnp.logical_not(present(WEST_EAST[side])))
        def _():
            edge_col[:, side] = jnp.zeros((ITERS,) + edge_col.shape[2:], F32)

    data[...] = jnp.zeros_like(data)
    first_moment[...] = jnp.zeros_like(first_moment)
    second_moment[...] = jnp.zeros_like(second_moment)

    def image_copies(slot):
        i, j = 1 - slot // 3, 1 - slot % 3
        return [
            pltpu.make_async_remote_copy(
                src_ref=own,
                dst_ref=around.at[slot],
                send_sem=image_send.at[0, slot],
                recv_sem=image_recv.at[0, slot],
                device_id=at((i, j)),
                device_id_type=MESH,
            )
        ]

    def field_copy(side):
        i, _ = NORTH_SOUTH[side]
        return pltpu.make_async_remote_copy(
            src_ref=field_hbm.at[:, pl.ds((tile_rows - HALO) * (1 - side), HALO), :],
            dst_ref=field_ref.at[:, pl.ds((HALO + tile_rows) * side, HALO), :],
            send_sem=field_send.at[side],
            recv_sem=field_recv.at[side],
            device_id=at((-i, 0)),
            device_id_type=MESH,
        )

    def disp_copy(step, side):
        _, j = WEST_EAST[side]
        return pltpu.make_async_remote_copy(
            src_ref=disp.at[step],
            dst_ref=edge_col.at[step, side],
            send_sem=disp_send.at[step, side],
            recv_sem=disp_recv.at[step, side],
            device_id=at((0, -j)),
            device_id_type=MESH,
        )

    def send_disp(step):
        for side in range(2):

            @pl.when(present(WEST_EAST[1 - side]))
            def _():
                disp_copy(step, side).start()

    for load in loads:
        load.wait()

    rows_near = 1 + (me_row > 0).astype(jnp.int32) + (me_row < rows_of_mesh - 1).astype(jnp.int32)
    cols_near = 1 + (me_col > 0).astype(jnp.int32) + (me_col < cols_of_mesh - 1).astype(jnp.int32)
    pl.semaphore_wait(barrier, rows_near * cols_near - 1)
    for i, j in AROUND:

        @pl.when(present((-i, -j)))
        def _():
            for copy in image_copies(3 * (i + 1) + j + 1):
                copy.start()

    for side in range(2):

        @pl.when(present(NORTH_SOUTH[1 - side]))
        def _():
            field_copy(side).start()

    sub64 = lax.broadcasted_iota(jnp.int32, (64, 128), 0)
    lane64 = lanes((64, 128))
    w2 = w2_ref[...].reshape(64, 9)
    for tap_col in range(3):
        spread = jnp.zeros((64, 128), F32)
        for tap_row in range(3):
            column = w2[:, 3 * tap_row + tap_col : 3 * tap_row + tap_col + 1]
            spread = jnp.where(
                lane64 == tap_row * 8 + (sub64 & 7), jnp.broadcast_to(column, (64, 128)), spread
            )
        base = jnp.sum(spread.reshape(8, 8, 128), axis=1)
        block = jnp.concatenate(
            [base if i == 0 else pltpu.roll(base, 8 * i, 1) for i in range(SLAB)], axis=0
        )
        high, low = split(block)
        at_row = tap_col * SLAB * 8
        toeplitz[at_row : at_row + SLAB * 8, 0:128] = high
        toeplitz[at_row : at_row + SLAB * 8, 128:256] = low
    w1 = w1_ref[...]
    taps = [jnp.broadcast_to(w1[:, k : k + 1], (8, 256)) for k in range(9)]
    sub8 = lax.broadcasted_iota(jnp.int32, (8, 256), 0)
    bias = jnp.zeros((8, 256), F32)
    for ch in range(CH):
        bias = jnp.where(sub8 == ch, b1_ref[ch], bias)

    for side in range(2):

        @pl.when(present(NORTH_SOUTH[side]))
        def _():
            field_copy(side).wait_recv()

    full_rows, full_cols = rows_of_mesh * tile_rows, cols_of_mesh * tile_cols
    row_ext = me_row * tile_rows - HALO + lax.broadcasted_iota(
        jnp.int32, (ext_rows, tile_cols), 0
    )
    in_section = (row_ext >= 0) & (row_ext < full_rows)
    for comp in range(2):
        raw[comp] = field_ref[comp]
        disp[0, comp] = jnp.where(in_section, REACH * jnp.tanh(field_ref[comp] / REACH), 0.0)
    send_disp(0)

    for i, j in AROUND:

        @pl.when(present((i, j)))
        def _():
            for copy in image_copies(3 * (i + 1) + j + 1):
                copy.wait_recv()

    lane_tile = lanes((80, 128))

    def encode(which, first_lane, first_row, row_margin, margin, slabs, store):
        def tile(slot):
            if slot == 4:
                return own[which].astype(F32)
            return around[slot, which].astype(F32)

        bands = []
        for col in range(3):
            bands.append(
                jnp.concatenate(
                    [tile(col)[8:, :], tile(3 + col), tile(6 + col)[: tile_rows - 8, :]], axis=0
                )
            )
        for tap_col in range(3):
            start = first_lane + tap_col
            if start == 128:
                left, right = bands[1], bands[2]
            else:
                turned = [pltpu.roll(x, 128 - start, 1) for x in bands]
                inside = lane_tile < 128 - start
                left = jnp.where(inside, turned[0], turned[1])
                right = jnp.where(inside, turned[1], turned[2])
            shifted[tap_col, :, 0:128] = left
            shifted[tap_col, :, 128:256] = right

        lane8 = lanes((8, 256))
        col8 = me_col * tile_cols + lane8 - (margin + 1)
        col_in = (col8 >= 0) & (col8 < full_cols)
        lane_e = lanes((SLAB * 8, 256))
        row_e = lax.broadcasted_iota(jnp.int32, (SLAB * 8, 256), 0) // 8
        col_e = me_col * tile_cols + lane_e - margin
        ok_col = (col_e >= 0) & (col_e < full_cols) & (lane_e < tile_cols + 2 * margin)

        for slab in slabs:
            hidden = []
            pixels = {}
            for i in range(SLAB + 4):
                for tap_col in range(3):
                    pixel = shifted[tap_col, pl.ds(first_row + slab + i, 1), :]
                    pixels[i, tap_col] = jnp.broadcast_to(pixel, (8, 256))
            for i in range(SLAB + 2):
                h = bias
                for tap in range(9):
                    h = h + taps[tap] * pixels[i + tap // 3, tap % 3]
                row = me_row * tile_rows + (slab + i - row_margin - 1)
                row_ok = (row >= 0) & (row < full_rows)
                row_factor = jnp.where(row_ok, 1.0, 0.0).astype(F32)
                hidden.append(jnp.where(col_in, jnp.maximum(h, 0.0) * row_factor, 0.0))
            high, low = split(jnp.concatenate(hidden, axis=0))
            t_high, t_low = toeplitz[:, 0:128], toeplitz[:, 128:256]
            product = dot(
                jnp.concatenate([t_high, t_high], axis=1), jnp.concatenate([high, low], axis=0)
            ) + dot(t_low, high)
            n = SLAB * 8
            embed = (
                product[0:n]
                + pltpu.roll(product[n : 2 * n], 255, 1)
                + pltpu.roll(product[2 * n : 3 * n], 254, 1)
            )
            row_abs = me_row * tile_rows + row_e + (slab - row_margin)
            embed = jnp.where(ok_col & (row_abs >= 0) & (row_abs < full_rows), embed, 0.0)
            store(slab, embed)

    def halves(even, odd, low_half):
        axis = even.ndim - 1
        return (
            jnp.where(low_half, even, pltpu.roll(odd, 64, axis)),
            jnp.where(low_half, pltpu.roll(even, 64, axis), odd),
        )

    low8 = lanes((8, 128)) < 64
    pairs = ext_rows // 2
    first_pair = (HALO - EXTRA) // 2

    def store_fixed(slab, embed):
        for pair in range(SLAB // 2):
            even = embed[pair * 16 : pair * 16 + 8, 0:128]
            odd = embed[pair * 16 + 8 : pair * 16 + 16, 0:128]
            left, right = halves(even, odd, low8)
            at_pair = first_pair + slab // 2 + pair
            fixed_embed[at_pair] = left
            fixed_embed[pairs + at_pair] = right

    low_e = lanes((SLAB * 8, 128)) < 64

    def store_moving(slab, embed):
        a, b = embed[:, 0:128], embed[:, 128:256]
        middle = jnp.where(low_e, pltpu.roll(a, 64, 1), pltpu.roll(b, 64, 1))
        for half, part in enumerate((a, middle)):
            lhs_f32[half, slab * 8 : (slab + SLAB) * 8, :] = part
            high, low = split(part)
            lhs[half, slab * 8 : (slab + SLAB) * 8, 0:128] = high
            lhs[half, slab * 8 : (slab + SLAB) * 8, 128:256] = low

    encode(0, 126, 24 - EXTRA - 2, EXTRA, 0, (0, 14, 22), store_fixed)
    encode(
        1, 109, 24 - EXTRA - REACH - 3, EXTRA + REACH + 1, REACH + 1, (0, 14, 28, 42, 56), store_moving
    )

    low_half = lanes((pairs, 128)) < 64
    lane_g = lanes((2 * pairs, 128))
    position = (lane_g & 63).astype(F32) + (REACH + 1)
    second_row = jnp.where(lane_g >= 64, 1.0, 0.0).astype(F32)

    def step(it, start, triples, unroll, last):
        grouped = []
        for comp in range(2):
            even = disp[it, comp, pl.ds(0, pairs, stride=2), :]
            odd = disp[it, comp, pl.ds(1, pairs, stride=2), :]
            grouped.append(jnp.concatenate(halves(even, odd, low_half), axis=0))
        for comp in range(2):
            nearest = jnp.floor(grouped[comp] + 0.5)
            f = grouped[comp] - nearest
            at_w = 6 * comp
            weights[at_w] = 0.5 * (0.5 - f) * (0.5 - f)
            weights[at_w + 1] = 0.75 - f * f
            weights[at_w + 2] = 0.5 * (0.5 + f) * (0.5 + f)
            weights[at_w + 3] = f - 0.5
            weights[at_w + 4] = -2.0 * f
            weights[at_w + 5] = 0.5 + f
            if comp == 0:
                weights[12] = nearest + REACH + second_row
            else:
                weights[13] = nearest + position

        place = lax.broadcasted_iota(jnp.int32, (128, 128), 0).astype(F32).astype(BF16)
        one_bf, zero_bf = jnp.ones((128, 128), BF16), jnp.zeros((128, 128), BF16)

        def sample(index, carry):
            half = index // triples
            triple = lax.rem(index, triples)
            first_group = half * pairs + start + triple * 3
            columns = []
            for j in range(2):
                target = weights[13, pl.ds(first_group + j, 1), :]
                for b in range(3):
                    hit = place == jnp.broadcast_to((target + (b - 1)).astype(BF16), (128, 128))
                    columns.append(jnp.where(hit, one_bf, zero_bf))
            onehot = jnp.concatenate(columns, axis=1)
            begin = (start - first_pair) * 16 + triple * 48
            window = lhs[half, pl.ds(pl.multiple_of(begin, 16), 304), :]
            picked = dot(window, jnp.concatenate([onehot, onehot], axis=0))
            target = weights[13, pl.ds(first_group + 2, 1), :]
            lane_of = [
                jnp.broadcast_to((target + (b - 1)).astype(jnp.int32), (8, 128)) for b in range(3)
            ]

            def column_tap(j, k, b):
                if j < 2:
                    n = 3 * j + b
                    return picked[(2 * j + k) * 8 : (2 * j + k) * 8 + 8, n * 128 : n * 128 + 128]
                row = lhs_f32[half, pl.ds(pl.multiple_of(begin + 32 + k * 8, 8), 8), :]
                return jnp.take_along_axis(row, lane_of[b], axis=1, mode="promise_in_bounds")

            for j in range(3):
                group = first_group + j

                def weight(k):
                    return jnp.broadcast_to(weights[k, pl.ds(group, 1), :], (8, 128))

                offset = weight(12)
                masks = []
                for shift in (17, 8, 4, 2, 1, 1):
                    mask = offset >= shift
                    masks.append(mask)
                    offset = jnp.where(mask, offset - shift, offset)
                taps_at = []
                for b in range(3):
                    rows = [column_tap(j, k, b) for k in range(36)]
                    for shift, mask, count in zip(
                        (17, 8, 4, 2, 1, 1), masks, (19, 11, 7, 5, 4, 3)
                    ):
                        rows = [jnp.where(mask, rows[k + shift], rows[k]) for k in range(count)]
                    taps_at.append(rows)
                warped = slope_row = slope_col = None
                w_row, dw_row = [weight(a) for a in range(3)], [weight(3 + a) for a in range(3)]
                for b in range(3):
                    along = sum(w_row[a] * taps_at[b][a] for a in range(3))
                    slant = sum(dw_row[a] * taps_at[b][a] for a in range(3))
                    w, dw = weight(6 + b), weight(9 + b)
                    terms = (w * along, w * slant, dw * along)
                    if b == 0:
                        warped, slope_row, slope_col = terms
                    else:
                        warped += terms[0]
                        slope_row += terms[1]
                        slope_col += terms[2]
                mismatch = warped - fixed_embed[group]
                data[0, pl.ds(group, 1), :] = jnp.sum(mismatch * slope_row, axis=0, keepdims=True)
                data[1, pl.ds(group, 1), :] = jnp.sum(mismatch * slope_col, axis=0, keepdims=True)
            return carry

        lax.fori_loop(0, 2 * triples, sample, 0, unroll=unroll)

        for side in range(2):

            @pl.when(present(WEST_EAST[side]))
            def _():
                disp_copy(it, side).wait_recv()

        lane = lanes((ext_rows, tile_cols))
        one = jnp.where(it == 0, 1 / (1 - 0.9), jnp.where(it == 1, 1 / (1 - 0.9**2), 1 / (1 - 0.9**3)))
        two = jnp.where(
            it == 0, 1 / (1 - 0.999), jnp.where(it == 1, 1 / (1 - 0.999**2), 1 / (1 - 0.999**3))
        )
        for comp in range(2):
            even, odd = halves(data[comp, 0:pairs, :], data[comp, pairs : 2 * pairs, :], low_half)
            unpaired[comp, pl.ds(0, pairs, stride=2), :] = even
            unpaired[comp, pl.ds(1, pairs, stride=2), :] = odd
            sampled = unpaired[comp] * (2.0 / CH)
            d = disp[it, comp]
            north = pltpu.roll(d, 1, 0)
            south = pltpu.roll(d, ext_rows - 1, 0)
            west = pltpu.roll(
                jnp.where(lane == tile_cols - 1, edge_col[it, 0, comp], d), 1, 1
            )
            east = pltpu.roll(
                jnp.where(lane == 0, edge_col[it, 1, comp], d), tile_cols - 1, 1
            )
            squashed = d * (1.0 / REACH)
            gradient = (
                sampled + 2.0 * stiffness * (4.0 * d - (south + north + east + west))
            ) * (1.0 - squashed * squashed)
            m1 = 0.9 * first_moment[comp] + 0.1 * gradient
            m2 = 0.999 * second_moment[comp] + 0.001 * gradient * gradient
            first_moment[comp] = m1
            second_moment[comp] = m2
            new = raw[comp] - step_size * (m1 * one) / (jnp.sqrt(m2 * two) + adam_epsilon)
            raw[comp] = new

            if not last:
                disp[it + 1, comp] = jnp.where(in_section, REACH * jnp.tanh(new / REACH), 0.0)

        if not last:
            send_disp(it + 1)

    def early(it, carry):
        step(it, first_pair, (tile_rows + 2 * EXTRA) // 6, 4, False)
        return carry

    lax.fori_loop(0, ITERS - 1, early, 0)
    step(ITERS - 1, first_pair, (tile_rows + 2 * EXTRA) // 6, 4, True)
    own_rows = slice(HALO, HALO + tile_rows)
    out_ref[...] = raw[:, own_rows, :] - field_ref[:, own_rows, :]
    for i, j in AROUND:

        @pl.when(present((-i, -j)))
        def _():
            for copy in image_copies(3 * (i + 1) + j + 1):
                copy.wait_send()

    for side in range(2):

        @pl.when(present(NORTH_SOUTH[1 - side]))
        def _():
            field_copy(side).wait_send()

        @pl.when(present(WEST_EAST[1 - side]))
        def _():
            for it in range(ITERS):
                disp_copy(it, side).wait_send()


def local(rows_of_mesh, cols_of_mesh, fixed, moving, field, w1, b1, w2):
    tile_rows, tile_cols = fixed.shape
    vmem = pl.BlockSpec(memory_space=pltpu.VMEM)
    tile = (tile_rows, tile_cols)
    ext = tile_rows + 2 * HALO
    return pl.pallas_call(
        functools.partial(kernel, rows_of_mesh, cols_of_mesh),
        out_shape=jax.ShapeDtypeStruct(field.shape, F32),
        in_specs=[pl.BlockSpec(memory_space=pltpu.HBM)] * 6,
        out_specs=vmem,
        scratch_shapes=[
            pltpu.VMEM((2, ext, tile_cols), F32),
            pltpu.VMEM(w1.shape, F32),
            pltpu.SMEM(b1.shape, F32),
            pltpu.VMEM(w2.shape, F32),
            pltpu.VMEM((2,) + tile, BF16),
            pltpu.VMEM((9, 2) + tile, BF16),
            pltpu.VMEM((3, 80, 256), F32),
            pltpu.VMEM((3 * SLAB * 8, 256), BF16),
            pltpu.VMEM((2, 70 * 8, 256), BF16),
            pltpu.VMEM((2, 70 * 8, 128), F32),
            pltpu.VMEM((ext, 8, 128), F32),
            pltpu.VMEM((ITERS, 2, ext, tile_cols), F32),
            pltpu.VMEM((ITERS, 2, 2, ext, tile_cols), F32),
            pltpu.VMEM((2, ext, tile_cols), F32),
            pltpu.VMEM((2, ext, tile_cols), F32),
            pltpu.VMEM((2, ext, tile_cols), F32),
            pltpu.VMEM((14, ext, 128), F32),
            pltpu.VMEM((2, ext, 128), F32),
            pltpu.VMEM((2, ext, 128), F32),
            pltpu.SemaphoreType.DMA((1, 9)),
            pltpu.SemaphoreType.DMA((1, 9)),
            pltpu.SemaphoreType.DMA((2,)),
            pltpu.SemaphoreType.DMA((2,)),
            pltpu.SemaphoreType.DMA((ITERS, 2)),
            pltpu.SemaphoreType.DMA((ITERS, 2)),
            pltpu.SemaphoreType.DMA((6,)),
        ],
        compiler_params=pltpu.CompilerParams(
            collective_id=0, has_side_effects=True, vmem_limit_bytes=32 << 20
        ),
        name="refine",
    )(*(pltpu.with_memory_space_constraint(x, pltpu.HBM) for x in (fixed, moving, field, w1, b1, w2)))


def solution(mesh):
    return jax.shard_map(
        functools.partial(local, mesh.shape["row"], mesh.shape["col"]),
        mesh=mesh,
        in_specs=(P("row", "col"), P("row", "col"), P(None, "row", "col"), P(), P(), P()),
        out_specs=P(None, "row", "col"),
        check_vma=False,
    )
```

time: 25.7 us -> 21.4 us (0.83)
  the two profiles are of different devices: /device:TPU:103 before, /device:TPU:121 now
where the time goes in v4:
time: 21.4 us; the launch traced here: 21.3 us
  Pallas kernels  20.7 us (97%)
  local copies, waits for them, and re-layouts  0.62 us (3%)
    pallas_call x1, Pallas kernels, local(): pl.pallas_call(functools.partial(kernel, rows_of_mesh, cols_of_mesh), out...  20.7 us
    unnamed x1, local copies, waits for them, and re-layouts  0.62 us

profile of v4, /device:TPU:121, one launch (start us, length us, event | category | flops | bytes accessed | tf_op | source)
XLA Modules:
  0.0 21.3 jit_solution(2668141522293916453)
XLA Ops:
  0.0 20.7 %refine.1 = f32[2,32,128]{2,1,0:T(8,128)S(1)} custom-call(bf16[32,128]{1,0:T(8,128)(2,1)} %fixed_hbm.1, bf16[32,128]{1,0:T(8,128)(2,1)} %moving_hbm.1, f32[2,32,128]{2,1,0:T(8,128)} %field_hbm.1, f32[8,9]{1,0:T(8,128)} %w1_hbm.1, f32[8]{0:T(128)} %b1_hbm.1, f32[8,8,9]{2,1,0:T(8,128)} %w2_hbm.1), custom_call_target="tpu_custom_call" | custom-call | tf_op jit(solution)/shard_map/refine/pallas_call | solution.py:513
  20.7 0.6 %copy.8 = f32[2,32,128]{2,1,0:T(8,128)} copy(f32[2,32,128]{2,1,0:T(8,128)S(1)} %refine.1) | data formatting | bytes 65536

commit v5 on v4

--- a/solution.py
+++ b/solution.py
@@ -18,7 +18,7 @@
 F32 = jnp.float32
 BF16 = jnp.bfloat16
 MESH = pl.DeviceIdType.MESH
-AROUND = [(i, j) for i in (-1, 0, 1) for j in (-1, 0, 1) if (i, j) != (0, 0)]
+AROUND = [(-1, -1), (-1, 1), (1, -1), (1, 1), (-1, 0), (1, 0), (0, -1), (0, 1)]
 NORTH_SOUTH = [(-1, 0), (1, 0)]
 WEST_EAST = [(0, -1), (0, 1)]
 HALO = 8
@@ -66,7 +66,7 @@
     first_moment,
     second_moment,
     weights,
-    data,
+    products,
     unpaired,
     image_send,
     image_recv,
@@ -127,7 +127,7 @@
         def _():
             edge_col[:, side] = jnp.zeros((ITERS,) + edge_col.shape[2:], F32)
 
-    data[...] = jnp.zeros_like(data)
+    products[...] = jnp.zeros_like(products)
     first_moment[...] = jnp.zeros_like(first_moment)
     second_moment[...] = jnp.zeros_like(second_moment)
 
@@ -430,8 +430,9 @@
                         slope_row += terms[1]
                         slope_col += terms[2]
                 mismatch = warped - fixed_embed[group]
-                data[0, pl.ds(group, 1), :] = jnp.sum(mismatch * slope_row, axis=0, keepdims=True)
-                data[1, pl.ds(group, 1), :] = jnp.sum(mismatch * slope_col, axis=0, keepdims=True)
+                at_group = pl.ds(pl.multiple_of(group * CH, CH), CH)
+                products[0, at_group, :] = mismatch * slope_row
+                products[1, at_group, :] = mismatch * slope_col
             return carry
 
         lax.fori_loop(0, 2 * triples, sample, 0, unroll=unroll)
@@ -448,7 +449,8 @@
             it == 0, 1 / (1 - 0.999), jnp.where(it == 1, 1 / (1 - 0.999**2), 1 / (1 - 0.999**3))
         )
         for comp in range(2):
-            even, odd = halves(data[comp, 0:pairs, :], data[comp, pairs : 2 * pairs, :], low_half)
+            summed = sum(products[comp, pl.ds(ch, 2 * pairs, stride=CH), :] for ch in range(CH))
+            even, odd = halves(summed[0:pairs], summed[pairs : 2 * pairs], low_half)
             unpaired[comp, pl.ds(0, pairs, stride=2), :] = even
             unpaired[comp, pl.ds(1, pairs, stride=2), :] = odd
             sampled = unpaired[comp] * (2.0 / CH)
@@ -479,11 +481,11 @@
             send_disp(it + 1)
 
     def early(it, carry):
-        step(it, first_pair, (tile_rows + 2 * EXTRA) // 6, 4, False)
+        step(it, first_pair, (tile_rows + 2 * EXTRA) // 6, 12, False)
         return carry
 
     lax.fori_loop(0, ITERS - 1, early, 0)
-    step(ITERS - 1, first_pair, (tile_rows + 2 * EXTRA) // 6, 4, True)
+    step(ITERS - 1, first_pair, (tile_rows + 2 * EXTRA) // 6, 12, True)
     own_rows = slice(HALO, HALO + tile_rows)
     out_ref[...] = raw[:, own_rows, :] - field_ref[:, own_rows, :]
     for i, j in AROUND:
@@ -533,7 +535,7 @@
             pltpu.VMEM((2, ext, tile_cols), F32),
             pltpu.VMEM((2, ext, tile_cols), F32),
             pltpu.VMEM((14, ext, 128), F32),
-            pltpu.VMEM((2, ext, 128), F32),
+            pltpu.VMEM((2, ext * CH, 128), F32),
             pltpu.VMEM((2, ext, 128), F32),
             pltpu.SemaphoreType.DMA((1, 9)),
             pltpu.SemaphoreType.DMA((1, 9)),

time: 21.4 us -> 20.9 us (0.977)
  Pallas kernels: 20.7 us -> 20.1 us
    pallas_call x1, Pallas kernels: 20.7 us -> 20.1 us  [local(): pl.pallas_call(functools.partial(kernel, rows_of_mesh, cols_of_mesh), out...]
where the time goes in v5:
time: 20.9 us; the launch traced here: 20.7 us
  Pallas kernels  20.1 us (96%)
  local copies, waits for them, and re-layouts  0.62 us (3%)
    pallas_call x1, Pallas kernels, local(): pl.pallas_call(functools.partial(kernel, rows_of_mesh, cols_of_mesh), out...  20.1 us
    unnamed x1, local copies, waits for them, and re-layouts  0.62 us

profile of v5, /device:TPU:121, one launch (start us, length us, event | category | flops | bytes accessed | tf_op | source)
XLA Modules:
  0.0 20.7 jit_solution(15158194490419851209)
XLA Ops:
  0.0 20.1 %refine.1 = f32[2,32,128]{2,1,0:T(8,128)S(1)} custom-call(bf16[32,128]{1,0:T(8,128)(2,1)} %fixed_hbm.1, bf16[32,128]{1,0:T(8,128)(2,1)} %moving_hbm.1, f32[2,32,128]{2,1,0:T(8,128)} %field_hbm.1, f32[8,9]{1,0:T(8,128)} %w1_hbm.1, f32[8]{0:T(128)} %b1_hbm.1, f32[8,8,9]{2,1,0:T(8,128)} %w2_hbm.1), custom_call_target="tpu_custom_call" | custom-call | tf_op jit(solution)/shard_map/refine/pallas_call | solution.py:515
  20.1 0.6 %copy.8 = f32[2,32,128]{2,1,0:T(8,128)} copy(f32[2,32,128]{2,1,0:T(8,128)S(1)} %refine.1) | data formatting | bytes 65536

commit v6 on v5

--- a/solution.py
+++ b/solution.py
@@ -61,6 +61,7 @@
     lhs_f32,
     fixed_embed,
     disp,
+    edges,
     edge_col,
     raw,
     first_moment,
@@ -158,7 +159,7 @@
     def disp_copy(step, side):
         _, j = WEST_EAST[side]
         return pltpu.make_async_remote_copy(
-            src_ref=disp.at[step],
+            src_ref=edges.at[step],
             dst_ref=edge_col.at[step, side],
             send_sem=disp_send.at[step, side],
             recv_sem=disp_recv.at[step, side],
@@ -166,7 +167,18 @@
             device_id_type=MESH,
         )
 
+    lane_edge = lanes((8, 128))
+    blocks = ext_rows // 8
+
     def send_disp(step):
+        first, last = jnp.zeros((8, 128), F32), jnp.zeros((8, 128), F32)
+        for n in range(2 * blocks):
+            at_row = n % blocks * 8
+            block = disp[step, n // blocks, at_row : at_row + 8, :]
+            first = jnp.where(lane_edge == n, pltpu.roll(block, n, 1) if n else block, first)
+            last = jnp.where(lane_edge == n, pltpu.roll(block, n + 1, 1), last)
+        edges[step, 0:8, :] = first
+        edges[step, 8:16, :] = last
         for side in range(2):
 
             @pl.when(present(WEST_EAST[1 - side]))
@@ -457,11 +469,15 @@
             d = disp[it, comp]
             north = pltpu.roll(d, 1, 0)
             south = pltpu.roll(d, ext_rows - 1, 0)
-            west = pltpu.roll(
-                jnp.where(lane == tile_cols - 1, edge_col[it, 0, comp], d), 1, 1
-            )
-            east = pltpu.roll(
-                jnp.where(lane == 0, edge_col[it, 1, comp], d), tile_cols - 1, 1
+            from_west, from_east = edge_col[it, 0, 8:16, :], edge_col[it, 1, 0:8, :]
+            tiles = range(comp * blocks, comp * blocks + blocks)
+            west_in = [pltpu.roll(from_west, 128 - n, 1) if n else from_west for n in tiles]
+            east_in = [pltpu.roll(from_east, 127 - n, 1) for n in tiles]
+            west = jnp.where(lane == 0, jnp.concatenate(west_in, axis=0), pltpu.roll(d, 1, 1))
+            east = jnp.where(
+                lane == tile_cols - 1,
+                jnp.concatenate(east_in, axis=0),
+                pltpu.roll(d, tile_cols - 1, 1),
             )
             squashed = d * (1.0 / REACH)
             gradient = (
@@ -530,7 +546,8 @@
             pltpu.VMEM((2, 70 * 8, 128), F32),
             pltpu.VMEM((ext, 8, 128), F32),
             pltpu.VMEM((ITERS, 2, ext, tile_cols), F32),
-            pltpu.VMEM((ITERS, 2, 2, ext, tile_cols), F32),
+            pltpu.VMEM((ITERS, 16, 128), F32),
+            pltpu.VMEM((ITERS, 2, 16, 128), F32),
             pltpu.VMEM((2, ext, tile_cols), F32),
             pltpu.VMEM((2, ext, tile_cols), F32),
             pltpu.VMEM((2, ext, tile_cols), F32),

time: 20.9 us -> 20.5 us (0.981)
  Pallas kernels: 20.1 us -> 19.7 us
    pallas_call x1, Pallas kernels: 20.1 us -> 19.7 us  [local(): pl.pallas_call(functools.partial(kernel, rows_of_mesh, cols_of_mesh), out...]
where the time goes in v6:
time: 20.5 us; the launch traced here: 20.3 us
  Pallas kernels  19.7 us (96%)
  local copies, waits for them, and re-layouts  0.62 us (3%)
    pallas_call x1, Pallas kernels, local(): pl.pallas_call(functools.partial(kernel, rows_of_mesh, cols_of_mesh), out...  19.7 us
    unnamed x1, local copies, waits for them, and re-layouts  0.62 us

profile of v6, /device:TPU:121, one launch (start us, length us, event | category | flops | bytes accessed | tf_op | source)
XLA Modules:
  0.0 20.3 jit_solution(3783358422062620455)
XLA Ops:
  0.0 19.7 %refine.1 = f32[2,32,128]{2,1,0:T(8,128)S(1)} custom-call(bf16[32,128]{1,0:T(8,128)(2,1)} %fixed_hbm.1, bf16[32,128]{1,0:T(8,128)(2,1)} %moving_hbm.1, f32[2,32,128]{2,1,0:T(8,128)} %field_hbm.1, f32[8,9]{1,0:T(8,128)} %w1_hbm.1, f32[8]{0:T(128)} %b1_hbm.1, f32[8,8,9]{2,1,0:T(8,128)} %w2_hbm.1), custom_call_target="tpu_custom_call" | custom-call | tf_op jit(solution)/shard_map/refine/pallas_call | solution.py:531
  19.7 0.6 %copy.8 = f32[2,32,128]{2,1,0:T(8,128)} copy(f32[2,32,128]{2,1,0:T(8,128)S(1)} %refine.1) | data formatting | bytes 65536

commit v7 on v6

--- a/solution.py
+++ b/solution.py
@@ -242,7 +242,7 @@
     in_section = (row_ext >= 0) & (row_ext < full_rows)
     for comp in range(2):
         raw[comp] = field_ref[comp]
-        disp[0, comp] = jnp.where(in_section, REACH * jnp.tanh(field_ref[comp] / REACH), 0.0)
+        disp[0, comp, 0:ext_rows, :] = jnp.where(in_section, REACH * jnp.tanh(field_ref[comp] / REACH), 0.0)
     send_disp(0)
 
     for i, j in AROUND:
@@ -465,8 +465,8 @@
             even, odd = halves(summed[0:pairs], summed[pairs : 2 * pairs], low_half)
             unpaired[comp, pl.ds(0, pairs, stride=2), :] = even
             unpaired[comp, pl.ds(1, pairs, stride=2), :] = odd
-            sampled = unpaired[comp] * (2.0 / CH)
-            d = disp[it, comp]
+            sampled = unpaired[comp, 0:ext_rows, :] * (2.0 / CH)
+            d = disp[it, comp, 0:ext_rows, :]
             north = pltpu.roll(d, 1, 0)
             south = pltpu.roll(d, ext_rows - 1, 0)
             from_west, from_east = edge_col[it, 0, 8:16, :], edge_col[it, 1, 0:8, :]
@@ -491,7 +491,7 @@
             raw[comp] = new
 
             if not last:
-                disp[it + 1, comp] = jnp.where(in_section, REACH * jnp.tanh(new / REACH), 0.0)
+                disp[it + 1, comp, 0:ext_rows, :] = jnp.where(in_section, REACH * jnp.tanh(new / REACH), 0.0)
 
         if not last:
             send_disp(it + 1)
@@ -545,15 +545,15 @@
             pltpu.VMEM((2, 70 * 8, 256), BF16),
             pltpu.VMEM((2, 70 * 8, 128), F32),
             pltpu.VMEM((ext, 8, 128), F32),
-            pltpu.VMEM((ITERS, 2, ext, tile_cols), F32),
+            pltpu.VMEM((ITERS, 2, ext + 8, tile_cols), F32),
             pltpu.VMEM((ITERS, 16, 128), F32),
             pltpu.VMEM((ITERS, 2, 16, 128), F32),
             pltpu.VMEM((2, ext, tile_cols), F32),
             pltpu.VMEM((2, ext, tile_cols), F32),
             pltpu.VMEM((2, ext, tile_cols), F32),
             pltpu.VMEM((14, ext, 128), F32),
-            pltpu.VMEM((2, ext * CH, 128), F32),
-            pltpu.VMEM((2, ext, 128), F32),
+            pltpu.VMEM((2, ext * CH + 8, 128), F32),
+            pltpu.VMEM((2, ext + 8, 128), F32),
             pltpu.SemaphoreType.DMA((1, 9)),
             pltpu.SemaphoreType.DMA((1, 9)),
             pltpu.SemaphoreType.DMA((2,)),

time: 20.5 us -> 20.5 us (level)
  no operation moved by 1% of the time
where the time goes in v7:
time: 20.5 us; the launch traced here: 20.3 us
  Pallas kernels  19.7 us (96%)
  local copies, waits for them, and re-layouts  0.62 us (3%)
    pallas_call x1, Pallas kernels, local(): pl.pallas_call(functools.partial(kernel, rows_of_mesh, cols_of_mesh), out...  19.7 us
    unnamed x1, local copies, waits for them, and re-layouts  0.62 us

profile of v7, /device:TPU:121, one launch (start us, length us, event | category | flops | bytes accessed | tf_op | source)
XLA Modules:
  0.0 20.3 jit_solution(13851011061017784969)
XLA Ops:
  0.0 19.7 %refine.1 = f32[2,32,128]{2,1,0:T(8,128)S(1)} custom-call(bf16[32,128]{1,0:T(8,128)(2,1)} %fixed_hbm.1, bf16[32,128]{1,0:T(8,128)(2,1)} %moving_hbm.1, f32[2,32,128]{2,1,0:T(8,128)} %field_hbm.1, f32[8,9]{1,0:T(8,128)} %w1_hbm.1, f32[8]{0:T(128)} %b1_hbm.1, f32[8,8,9]{2,1,0:T(8,128)} %w2_hbm.1), custom_call_target="tpu_custom_call" | custom-call | tf_op jit(solution)/shard_map/refine/pallas_call | solution.py:531
  19.7 0.6 %copy.8 = f32[2,32,128]{2,1,0:T(8,128)} copy(f32[2,32,128]{2,1,0:T(8,128)S(1)} %refine.1) | data formatting | bytes 65536
